TPU v7x, 128 devices: a whole 4x4x4 slice. The times are simulated.
128 devices in a mesh: seq: 8 (over z, core), exp: 16 (over y, x).
Axes of the slice: x: 4, y: 4, z: 4, core: 2. Of those that a mesh axis runs over, the one named last changes fastest.
Arguments:
- tokens: bfloat16 [32768, 4096], P(('seq', 'exp')), may hold values from -3 to 3
- cotangent: bfloat16 [32768, 4096], P(('seq', 'exp')), may hold values from -2 to 2
- router: bfloat16 [4096, 16], replicated, may hold values from -0.09375 to 0.09375
- threshold: float32 [16], replicated, may hold values from -1 to 1
- w_gate: bfloat16 [16, 4096, 1536], P('exp', None, 'seq'), may hold values from -0.09375 to 0.09375
- w_up: bfloat16 [16, 4096, 1536], P('exp', None, 'seq'), may hold values from -0.09375 to 0.09375
- w_down: bfloat16 [16, 1536, 4096], P('exp', 'seq'), may hold values from -0.15625 to 0.15625
- hid_scale: float32 [16, 1536], P('exp', 'seq'), may hold values from 0.5 to 2
- picks: int32 [128, 16, 4], P(('seq', 'exp')), may hold values from 0 to 255, as said below
- counts: int32 [128, 16], P(('seq', 'exp')), may hold values from 1 to 4, as said below
Outputs:
- mixture: bfloat16 [32768, 4096], P(('seq', 'exp'))
- token_grad: bfloat16 [32768, 4096], P(('seq', 'exp'))
- router_grad: float32 [4096, 16], P(('seq', 'exp'))
- threshold_grad: float32 [16], replicated
- gate_grad: float32 [16, 4096, 1536], P('exp', None, 'seq')
- up_grad: float32 [16, 4096, 1536], P('exp', None, 'seq')
- down_grad: float32 [16, 1536, 4096], P('exp', 'seq')
Inputs may be any that keep to these rules, and one draw needn't show every extreme that they name: Each list picks[p, e] holds 4 distinct local rows of owner p. `counts`: for every expert some owner fills all 4 slots.
All inputs are finite; a program needn't handle non-finite values.
Results may differ from a plain program's by a relative error of at most 0.018.
Values may be sent and summed in bfloat16 or wider, within the bound.
A program may use at most 128 MiB of HBM per device.

v0:
```python
import jax
import jax.numpy as jnp
from jax import lax
from jax.sharding import PartitionSpec as P


def on_device(tokens, cotangent, router, threshold, w_gate, w_up, w_down, hid_scale, picks, counts):
    experts = router.shape[1]
    slot_count = picks.shape[2]
    features = tokens.shape[1]
    row_count = tokens.shape[0]
    seq_count = lax.axis_size("seq")
    chosen = picks[0]
    active = (jnp.arange(slot_count, dtype=jnp.int32)[None, :] < counts[0][:, None]).astype(
        jnp.float32
    )
    scores = jnp.dot(tokens, router, preferred_element_type=jnp.float32)
    gates_all = jax.nn.sigmoid(scores - threshold[None, :])
    column = jnp.broadcast_to(jnp.arange(experts, dtype=jnp.int32)[:, None], (experts, slot_count))
    raw_gate = gates_all[chosen, column]
    gate_value = raw_gate * active
    picked_rows = tokens[chosen]
    picked_cot = cotangent[chosen].astype(jnp.float32)
    scaled_cot = (picked_cot * gate_value[:, :, None]).astype(jnp.bfloat16)
    stacked = jnp.stack([picked_rows, scaled_cot], axis=1)
    copies = jnp.tile(stacked, (seq_count, 1, 1, 1))
    arrived = lax.all_to_all(copies, ("seq", "exp"), split_axis=0, concat_axis=2, tiled=True)
    expert_rows = arrived[0, 0]
    expert_cot = arrived[0, 1]
    gate_mat = w_gate[0]
    up_mat = w_up[0]
    down_mat = w_down[0]
    scale_row = hid_scale[0][None, :]
    pre_gate = jnp.dot(expert_rows, gate_mat, preferred_element_type=jnp.float32)
    pre_up = jnp.dot(expert_rows, up_mat, preferred_element_type=jnp.float32)
    sigmoid_val = jax.nn.sigmoid(pre_gate)
    activated = pre_gate * sigmoid_val
    hidden = (activated * pre_up * scale_row).astype(jnp.bfloat16)
    scaled_grad = jnp.dot(expert_cot, down_mat.T, preferred_element_type=jnp.float32) * scale_row
    gate_delta = (
        scaled_grad * pre_up * sigmoid_val * (1.0 + pre_gate * (1.0 - sigmoid_val))
    ).astype(jnp.bfloat16)
    up_delta = (scaled_grad * activated).astype(jnp.bfloat16)
    contract_rows = (((0,), (0,)), ((), ()))
    down_grad = lax.dot_general(
        hidden, expert_cot, contract_rows, preferred_element_type=jnp.float32
    )
    gate_grad = lax.dot_general(
        expert_rows, gate_delta, contract_rows, preferred_element_type=jnp.float32
    )
    up_grad = lax.dot_general(
        expert_rows, up_delta, contract_rows, preferred_element_type=jnp.float32
    )
    out_mine = lax.psum_scatter(
        jnp.dot(hidden, down_mat, preferred_element_type=jnp.float32).astype(jnp.bfloat16),
        "seq",
        scatter_dimension=0,
        tiled=True,
    )
    contract_hidden = (((1,), (1,)), ((), ()))
    first_term = lax.dot_general(
        gate_delta, gate_mat, contract_hidden, preferred_element_type=jnp.float32
    )
    grad_mine = lax.psum_scatter(
        (
            first_term
            + lax.dot_general(up_delta, up_mat, contract_hidden, preferred_element_type=jnp.float32)
        ).astype(jnp.bfloat16),
        "seq",
        scatter_dimension=0,
        tiled=True,
    )
    packed = jnp.stack([out_mine, grad_mine]).reshape(2, experts, slot_count, features)
    returned = lax.all_to_all(packed, "exp", split_axis=1, concat_axis=1, tiled=True)
    out_wide = returned[0].astype(jnp.float32)
    flat_index = chosen.reshape(-1)
    mixture = (
        jnp.zeros((row_count, features), jnp.float32)
        .at[flat_index]
        .add((gate_value[:, :, None] * out_wide).reshape(-1, features))
    )
    gate_pull = active * jnp.sum(picked_cot * out_wide, axis=-1)
    score_pick = gate_pull * raw_gate * (1.0 - raw_gate)
    score_grad = jnp.zeros((row_count, experts), jnp.float32).at[chosen, column].add(score_pick)
    token_grad = (
        jnp.zeros((row_count, features), jnp.float32)
        .at[flat_index]
        .add(returned[1].astype(jnp.float32).reshape(-1, features))
    )
    token_grad = token_grad + jnp.dot(
        score_grad, router.astype(jnp.float32).T, precision=lax.Precision.HIGHEST
    )
    router_term = jnp.dot(tokens.astype(jnp.float32).T, score_grad, precision=lax.Precision.HIGHEST)
    router_grad = lax.psum_scatter(router_term, ("seq", "exp"), scatter_dimension=0, tiled=True)
    threshold_grad = -lax.psum(jnp.sum(score_grad, axis=0), ("seq", "exp"))
    return (
        mixture.astype(jnp.bfloat16),
        token_grad.astype(jnp.bfloat16),
        router_grad,
        threshold_grad,
        gate_grad[None],
        up_grad[None],
        down_grad[None],
    )


def solution(mesh):
    placed = (
        P(("seq", "exp"), None),
        P(("seq", "exp"), None),
        P(),
        P(),
        P("exp", None, "seq"),
        P("exp", None, "seq"),
        P("exp", "seq", None),
        P("exp", "seq"),
        P(("seq", "exp"), None, None),
        P(("seq", "exp"), None),
    )
    return jax.shard_map(
        on_device,
        mesh=mesh,
        in_specs=placed,
        out_specs=(
            P(("seq", "exp"), None),
            P(("seq", "exp"), None),
            P(("seq", "exp"), None),
            P(),
            P("exp", None, "seq"),
            P("exp", None, "seq"),
            P("exp", "seq", None),
        ),
        check_vma=False,
    )
```

profile of v0, /device:TPU:0, one launch (start us, length us, event | category | flops | bytes accessed | tf_op | source)
XLA Modules:
  0.0 933.7 jit_solution(11691473644793321143)
XLA Ops:
  8.8 1.6 fusion.28
  12.2 3.2 gather_fusion.2
  19.3 1.8 pad_maximum_fusion
  22.3 7.8 tile.4
  30.0 107.0 %all_to_all.23 = bf16[128,2,4,4096]{3,1,2,0:T(2,128)(2,1)S(1)} all-to-all(bf16[128,2,4,4096]{3,1,2,0:T(2,128)(2,1)S(1)} %bitcast.91), channel_id=1, replica_groups=mesh['seq'=8,'exp'=16] {'seq','exp'}, dimensions={0} | all-to-all | bytes 16777216 | tf_op jit(solution)/shard_map/all_to_all | solution.py:27
  137.0 13.0 %fusion.39 = (bf16[1,1,512,4096]{3,1,2,0:T(2,128)(2,1)}, bf16[1,1,512,4096]{3,1,2,0:T(2,128)(2,1)S(1)}) fusion(bf16[1,2,512,4096]{3,1,2,0:T(2,128)(2,1)S(1)} %bitcast.90), kind=kLoop, calls=%fused_computation.67 | loop fusion | bytes 16777216 | tf_op jit(solution)/shard_map/slice | solution.py:29
  150.0 4.8 copy.41
  157.4 8.2 fusion.20
  165.7 1.8 multiply_convert_fusion.3
  167.5 3.2 convolution_convert_fusion
  170.9 2.8 fusion.17
  173.7 3.2 add_convert_fusion
  179.4 27.0 %reduce-scatter.6.cloned.1.call-done = bf16[64,4096]{1,0:T(8,128)(2,1)} async-done(((bf16[512,4096]{1,0:T(8,128)(2,1)}), bf16[64,4096]{1,0:T(8,128)(2,1)}) %reduce-scatter.6.cloned.1.call-update) | async-done | bytes 524304 | tf_op jit(solution)/shard_map/reduce_scatter | solution.py:54
  207.6 38.1 %reduce-scatter.8.cloned.1.call-done = bf16[64,4096]{1,0:T(8,128)(2,1)} async-done(((bf16[512,4096]{1,0:T(8,128)(2,1)}), bf16[64,4096]{1,0:T(8,128)(2,1)}) %reduce-scatter.8.cloned.1.call-update) | async-done | bytes 524304 | tf_op jit(solution)/shard_map/reduce_scatter | solution.py:64
  247.0 1.6 pad_maximum_fusion.1
  248.6 6.8 all-to-all-start.1
  255.5 5.1 convolution_bitcast_fusion.1
  260.6 2.7 convolution_bitcast_fusion
  263.4 6.7 convolution_bitcast_fusion.2
  270.1 1.6 fusion.29
  271.9 3.9 scatter_fusion
  276.9 1.9 copy.39
  278.8 1.6 slice_convert_fusion
  280.4 67.3 %psum.7 = f32[16]{0:T(128)S(1)} all-reduce(f32[16]{0:T(128)S(1)} %reduce_sum.19), channel_id=1, replica_groups=mesh['seq'=8,'exp'=16] {'seq','exp'}, use_global_device_ids=true, to_apply=%region_8.0 | all-reduce | flops 16 | bytes 128 | tf_op jit(solution)/shard_map/psum | solution.py:95
  348.2 1.6 reshape.196
  349.8 2.6 reshape.153
  352.3 4.9 scatter_custom_fusion
  357.2 3.8 convert_element_type.78
  361.1 3.8 fusion.40
  364.8 6.0 scatter_fusion.1
  370.9 3.8 convert_element_type.84
  374.6 550.7 %reduce-scatter.10.cloned.1.call-done = f32[32,16]{1,0:T(8,128)} async-done(((f32[4096,16]{1,0:T(8,128)}), f32[32,16]{1,0:T(8,128)}) %reduce-scatter.10.cloned.1.call-update) | async-done | bytes 2064
  (71 shorter events, 19.3 us)
Async XLA Ops:
  7.2 1.6 copy-start
  7.2 199.2 %reduce-scatter.6.cloned.1.call-start = ((), (), s32[]{:S(2)}) async-start(), calls=%async_computation.5 | async-start | bytes 4718592 | tf_op jit(solution)/shard_map/reduce_scatter | solution.py:54
  12.2 5.5 copy-start.12
  150.0 4.8 copy-start.3
  154.8 10.8 %copy-start.1 = (bf16[1,1,512,4096]{3,2,1,0:T(8,128)(2,1)}, bf16[1,1,512,4096]{3,2,1,0:T(8,128)(2,1)S(1)}, u32[]{:S(2)}) copy-start(bf16[1,1,512,4096]{3,2,1,0:T(8,128)(2,1)S(1)} %copy.41) | copy-start | bytes 12582916
  154.8 2.6 copy-start.6
  154.8 2.6 copy-start.13
  157.4 8.3 copy-start.4
  167.5 3.3 copy-start.9
  167.5 6.2 copy-start.7
  170.8 75.0 %reduce-scatter.8.cloned.1.call-start = ((), (), s32[]{:S(2)}) async-start(), calls=%async_computation.6 | async-start | bytes 4718592 | tf_op jit(solution)/shard_map/reduce_scatter | solution.py:64
  170.9 2.8 copy-start.5
  177.0 0.7 copy-start.11
  248.6 21.5 %all-to-all-start.1 = ((bf16[2,16,4,4096]{3,2,0,1:T(4,128)(2,1)}), bf16[2,16,4,4096]{3,2,0,1:T(4,128)(2,1)S(1)}, u32[]{:S(2)}, u32[]{:S(2)}) async-start(bf16[2,16,4,4096]{3,2,0,1:T(4,128)(2,1)} %pad_maximum_fusion.1), calls=%async_computation.3 | async-start | bytes 2097152 | tf_op jit(solution)/shard_map/all_to_all | solution.py:74
  255.4 669.9 %reduce-scatter.10.cloned.1.call-start = ((), (), s32[]{:S(2)}) async-start(), calls=%async_computation.7 | async-start | bytes 2113536
  255.5 5.1 copy-start.2
  255.5 5.1 copy-start.8
  255.5 7.8 slice-start
  260.6 2.8 slice-start.1
  357.2 3.8 copy-start.10
Sparse Core Ops, SparseCore 0:
  170.9 35.4 reduce-scatter.5
  208.8 36.9 reduce-scatter.7
  278.9 646.3 reduce-scatter.9
where the time goes:
time: 945 us; the launch traced here: 934 us
  waiting for transfers between devices  616 us (65%)
  blocking collectives  174 us (18%)
  local copies, waits for them, and re-layouts  48.3 us (5%)
  matrix products  41.6 us (4%)
  other arithmetic  32.2 us (3%)
  between operations  14.5 us (2%)
    unnamed x4, waiting for transfers between devices  551 us
    all_to_all x1, blocking collectives, on_device(): lax.all_to_all(copies, ('seq', 'exp'), split_axis=0, concat_axis=2, tiled...  107 us
    psum x1, blocking collectives, on_device(): threshold_grad = -lax.psum(jnp.sum(score_grad, axis=0), ('seq', 'exp'))  67.3 us
    reduce_scatter x1, waiting for transfers between devices, on_device(): lax.psum_scatter((first_term + lax.dot_general(up_delta, up_mat, contract...  38.1 us
    reduce_scatter x1, waiting for transfers between devices, on_device(): lax.psum_scatter(jnp.dot(hidden, down_mat, preferred_element_type=jnp.flo...  27 us
  transfers between devices with their start and end apart: 4, of which 3 were waited for; matrix products, arithmetic and copies ran while one was open for 6% of the time, Pallas kernels for 0%

commit v1 on v0

v1 whole, which is shorter than its diff:
```python
import jax
import jax.numpy as jnp
from jax import lax
from jax.experimental import pallas as pl
from jax.experimental.pallas import tpu as pltpu
from jax.sharding import PartitionSpec as P

MESH = pl.DeviceIdType.MESH
BF = jnp.bfloat16
F32 = jnp.float32
HIGH = lax.Precision.HIGHEST
UP = (0, 2)
DOWN = (1, 3)


class Spot:
    def __init__(self):
        self.s = lax.axis_index("seq")
        self.e = lax.axis_index("exp")
        self.z = lax.div(self.s, 2)
        self.c = lax.rem(self.s, 2)
        self.y = lax.div(self.e, 4)
        self.x = lax.rem(self.e, 4)
        self.partner = (self.s + 1 - 2 * self.c, self.e)
        self.above = (self.layer(1) * 2 + self.c, self.e)
        self.below = (self.layer(3) * 2 + self.c, self.e)

    def layer(self, up):
        return lax.rem(self.z + up, 4)

    def group(self, i):
        return lax.rem(self.y + i, 4)

    def slot(self, up, other, i):
        core = self.c + other * (1 - 2 * self.c)
        return (self.layer(up) * 2 + core) * 4 + self.group(i)

    def plane_peers(self):
        return [(self.s, lax.rem(self.e + d, 16)) for d in range(1, 16)]

    def column_peers(self):
        return [(lax.rem(self.s + d, 8), self.e) for d in range(1, 8)]


def greet(peers):
    for peer in peers:
        pl.semaphore_signal(
            pltpu.get_barrier_semaphore(), inc=1, device_id=peer, device_id_type=MESH
        )


def greeted(count):
    pl.semaphore_wait(pltpu.get_barrier_semaphore(), count)


def push(src, dst, send_sem, recv_sem, device):
    copy = pltpu.make_async_remote_copy(
        src_ref=src,
        dst_ref=dst,
        send_sem=send_sem,
        recv_sem=recv_sem,
        device_id=device,
        device_id_type=MESH,
    )
    copy.start()
    return copy


def landed(dst, recv_sem, device):
    pltpu.make_async_remote_copy(
        src_ref=dst,
        dst_ref=dst,
        send_sem=recv_sem,
        recv_sem=recv_sem,
        device_id=device,
        device_id_type=MESH,
    ).wait_recv()


def dispatch_kernel(xr, cr, xc, msg, buf, s1, r1, sp, rp, sm, rm, sq, rq, own):
    at = Spot()
    peers = at.plane_peers()
    greet(peers + [at.partner, at.above, at.below])
    for e in range(16):
        msg[e, 0] = xr[4 * e : 4 * e + 4, :]
        msg[e, 1] = cr[4 * e : 4 * e + 4, :]
    greeted(18)
    sent = []
    for d, peer in enumerate(peers):
        sent.append(push(msg.at[peer[1]], buf.at[at.e], s1.at[d], r1.at[d], peer))
    mine = pltpu.make_async_copy(msg.at[at.e], buf.at[at.e], own)
    mine.start()
    mine.wait()

    def hand_over(slot, q):
        sent.append(push(xc.at[:, slot], xc.at[:, slot], sq.at[q], rq.at[q], at.partner))

    def climb(slot, k):
        sent.append(push(xc.at[:, slot], xc.at[:, slot], sp.at[k], rp.at[k], at.above))

    def sink(slot, k):
        sent.append(push(xc.at[:, slot], xc.at[:, slot], sm.at[k], rm.at[k], at.below))

    for i in range(4):
        group = at.group(i)
        slot = at.slot(0, 0, i)
        for x in range(4):
            origin = group * 4 + x
            behind = lax.rem(at.e - origin + 16, 16)

            @pl.when(behind > 0)
            def _():
                landed(buf.at[origin], r1.at[behind - 1], peers[0])

        for x in range(4):
            for a in range(2):
                xc[a, slot, 4 * x : 4 * x + 4, :] = buf[group * 4 + x, a]
        climb(slot, i)
        sink(slot, i)
        hand_over(slot, i)
    for i in range(4):
        slot = at.slot(3, 0, i)
        landed(xc.at[:, slot], rp.at[i], at.above)
        if i in UP:
            climb(slot, 4 + UP.index(i))
        hand_over(slot, 4 + i)
        slot = at.slot(1, 0, i)
        landed(xc.at[:, slot], rm.at[i], at.below)
        if i in DOWN:
            sink(slot, 4 + DOWN.index(i))
        hand_over(slot, 8 + i)
    for i in range(4):
        slot = at.slot(2, 0, i)
        if i in UP:
            landed(xc.at[:, slot], rp.at[4 + UP.index(i)], at.above)
        else:
            landed(xc.at[:, slot], rm.at[4 + DOWN.index(i)], at.below)
        hand_over(slot, 12 + i)
    for q in range(16):
        up = (0, 3, 1, 2)[q // 4]
        landed(xc.at[:, at.slot(up, 1, q % 4)], rq.at[q], at.partner)
    for copy in sent:
        copy.wait_send()


def dispatch(rows, cots):
    width = rows.shape[1]
    vmem = pl.BlockSpec(memory_space=pltpu.VMEM)
    dma = pltpu.SemaphoreType.DMA
    return pl.pallas_call(
        dispatch_kernel,
        out_shape=jax.ShapeDtypeStruct((2, 32, 16, width), BF),
        in_specs=[vmem, vmem],
        out_specs=vmem,
        scratch_shapes=[
            pltpu.VMEM((16, 2, 4, width), BF),
            pltpu.VMEM((16, 2, 4, width), BF),
            dma((15,)), dma((15,)), dma((6,)), dma((6,)), dma((6,)), dma((6,)),
            dma((16,)), dma((16,)), dma,
        ],
        compiler_params=pltpu.CompilerParams(
            collective_id=0, has_side_effects=True, vmem_limit_bytes=60 << 20
        ),
    )(rows, cots)


def total(dst, parts):
    width = parts[0].shape[-1]
    step = 512

    def body(j, carry):
        cols = pl.ds(pl.multiple_of(j * step, step), step)
        acc = parts[0][:, :, cols].astype(F32)
        for part in parts[1:]:
            acc = acc + part[:, :, cols].astype(F32)
        dst[:, :, cols] = acc.astype(BF)
        return carry

    lax.fori_loop(0, width // step, body, 0)


def return_kernel(
    p, ret, pb, xp, xm, tot, om, rb, sq, rq, sp, rp, sm, rm, s3, r3, own
):
    at = Spot()
    peers = at.plane_peers()
    greet(peers + [at.partner, at.above, at.below])
    greeted(18)
    order = (
        [(1, i) for i in DOWN] + [(3, i) for i in UP] + [(2, i) for i in range(4)]
        + [(1, i) for i in UP] + [(3, i) for i in DOWN] + [(0, i) for i in range(4)]
    )
    sent = []
    for up, i in order:
        q = up * 4 + i
        slot = at.slot(up, 1, i)
        sent.append(push(p.at[:, slot], pb.at[q], sq.at[q], rq.at[q], at.partner))

    def climb(src, k):
        sent.append(push(src, xp.at[k], sp.at[k], rp.at[k], at.above))

    def sink(src, k):
        sent.append(push(src, xm.at[k], sm.at[k], rm.at[k], at.below))

    for up, i in order:
        q = up * 4 + i
        slot = at.slot(up, 0, i)
        landed(pb.at[q], rq.at[q], at.partner)
        parts = [p.at[:, slot], pb.at[q]]
        if up == 1 and i in UP:
            k = 2 + UP.index(i)
            landed(xp.at[k], rp.at[k], at.above)
            parts.append(xp.at[k])
        if up == 3 and i in DOWN:
            k = 2 + DOWN.index(i)
            landed(xm.at[k], rm.at[k], at.below)
            parts.append(xm.at[k])
        if up == 0:
            ku = UP.index(i) + 4 if i in UP else DOWN.index(i)
            kd = UP.index(i) if i in UP else DOWN.index(i) + 4
            landed(xp.at[ku], rp.at[ku], at.above)
            landed(xm.at[kd], rm.at[kd], at.below)
            parts += [xp.at[ku], xm.at[kd]]
        total(tot.at[q], parts)
        if up == 1:
            climb(tot.at[q], UP.index(i) + 4 if i in UP else DOWN.index(i))
        if up == 3:
            sink(tot.at[q], UP.index(i) if i in UP else DOWN.index(i) + 4)
        if up == 2:
            if i in UP:
                climb(tot.at[q], 2 + UP.index(i))
            else:
                sink(tot.at[q], 2 + DOWN.index(i))
        if up == 0:
            group = at.group(i)
            for x in range(4):
                for a in range(2):
                    om[i * 4 + x, a] = tot[q, a, 4 * x : 4 * x + 4, :]
            for x in range(4):
                m = i * 4 + x
                target = group * 4 + x
                ahead = lax.rem(target - at.e + 16, 16)

                def go():
                    return pltpu.make_async_remote_copy(
                        src_ref=om.at[m],
                        dst_ref=rb.at[at.e],
                        send_sem=s3.at[m],
                        recv_sem=r3.at[ahead - 1],
                        device_id=(at.s, target),
                        device_id_type=MESH,
                    )

                @pl.when(ahead > 0)
                def _():
                    go().start()

                @pl.when(ahead == 0)
                def _():
                    mine = pltpu.make_async_copy(om.at[m], rb.at[at.e], own)
                    mine.start()
                    mine.wait()

    for e in range(16):
        behind = lax.rem(at.e - e + 16, 16)

        @pl.when(behind > 0)
        def _():
            landed(rb.at[e], r3.at[behind - 1], peers[0])

        for a in range(2):
            ret[a, 4 * e : 4 * e + 4, :] = rb[e, a]
    for i in range(4):
        for x in range(4):
            m = i * 4 + x
            target = at.group(i) * 4 + x
            ahead = lax.rem(target - at.e + 16, 16)

            @pl.when(ahead > 0)
            def _():
                pltpu.make_async_remote_copy(
                    src_ref=om.at[m],
                    dst_ref=rb.at[at.e],
                    send_sem=s3.at[m],
                    recv_sem=r3.at[ahead - 1],
                    device_id=(at.s, target),
                    device_id_type=MESH,
                ).wait_send()

    for copy in sent:
        copy.wait_send()


def give_back(parts):
    width = parts.shape[-1]
    vmem = pl.BlockSpec(memory_space=pltpu.VMEM)
    dma = pltpu.SemaphoreType.DMA
    return pl.pallas_call(
        return_kernel,
        out_shape=jax.ShapeDtypeStruct((2, 64, width), BF),
        in_specs=[vmem],
        out_specs=vmem,
        scratch_shapes=[
            pltpu.VMEM((16, 2, 16, width), BF),
            pltpu.VMEM((6, 2, 16, width), BF),
            pltpu.VMEM((6, 2, 16, width), BF),
            pltpu.VMEM((16, 2, 16, width), BF),
            pltpu.VMEM((16, 2, 4, width), BF),
            pltpu.VMEM((16, 2, 4, width), BF),
            dma((16,)), dma((16,)), dma((6,)), dma((6,)), dma((6,)), dma((6,)),
            dma((16,)), dma((15,)), dma,
        ],
        compiler_params=pltpu.CompilerParams(
            collective_id=1, has_side_effects=True, vmem_limit_bytes=60 << 20
        ),
    )(parts)


def reduce_kernel(t, out, a, b, ext, sa, ra, sb, rb):
    at = Spot()
    column = at.column_peers()
    plane = at.plane_peers()
    greet(column + plane)
    greeted(22)
    sent = []
    for d, peer in enumerate(column):
        sent.append(push(t.at[peer[0]], a.at[d], sa.at[d], ra.at[d], peer))
    acc = t[at.s]
    for d in range(7):
        landed(a.at[d], ra.at[d], column[d])
        acc = acc + a[d]
    for y in range(4):
        ext[y, 0:16, :] = acc[0:16, 128 * y : 128 * y + 128]
        ext[y, 16:24, :] = acc[16:24, 0:128]
    for d, peer in enumerate(plane):
        sent.append(push(ext.at[lax.div(peer[1], 4)], b.at[d], sb.at[d], rb.at[d], peer))
    done = ext[at.y]
    th = done[16:24, :]
    res = done[0:16, :]
    for d in range(15):
        landed(b.at[d], rb.at[d], plane[d])
        res = res + b[d, 0:16, :]
        th = th + b[d, 16:24, :]
    out[0:16, :] = res
    out[16:24, :] = th
    for copy in sent:
        copy.wait_send()


def reduce_all(t):
    vmem = pl.BlockSpec(memory_space=pltpu.VMEM)
    dma = pltpu.SemaphoreType.DMA
    return pl.pallas_call(
        reduce_kernel,
        out_shape=jax.ShapeDtypeStruct((24, 128), F32),
        in_specs=[vmem],
        out_specs=vmem,
        scratch_shapes=[
            pltpu.VMEM((7, 24, 512), F32),
            pltpu.VMEM((15, 24, 128), F32),
            pltpu.VMEM((4, 24, 128), F32),
            dma((7,)), dma((7,)), dma((15,)), dma((15,)),
        ],
        compiler_params=pltpu.CompilerParams(collective_id=2, has_side_effects=True),
    )(t)


def on_device(tokens, cotangent, router, threshold, w_gate, w_up, w_down, hid_scale, picks, counts):
    experts = router.shape[1]
    slot_count = picks.shape[2]
    features = tokens.shape[1]
    row_count = tokens.shape[0]
    chosen = picks[0]
    active = (jnp.arange(slot_count, dtype=jnp.int32)[None, :] < counts[0][:, None]).astype(F32)
    scores = jnp.dot(tokens, router, preferred_element_type=F32)
    gates_all = jax.nn.sigmoid(scores - threshold[None, :])
    select = (
        chosen.reshape(-1)[:, None] == jnp.arange(row_count, dtype=jnp.int32)[None, :]
    )
    select_bf = select.astype(BF)
    select_f = select.astype(F32)
    gates_wide = jnp.repeat(gates_all.T, slot_count, axis=0)
    raw_gate = jnp.sum(jnp.where(select, gates_wide, 0.0), axis=1)
    live = active.reshape(-1)
    gate_value = raw_gate * live
    picked_rows = jnp.dot(select_bf, tokens, preferred_element_type=F32).astype(BF)
    picked_cot = jnp.dot(select_bf, cotangent, preferred_element_type=F32)
    scaled_cot = (picked_cot * gate_value[:, None]).astype(BF)
    arrived = dispatch(picked_rows, scaled_cot)
    expert_rows = arrived[0].reshape(-1, features)
    expert_cot = arrived[1].reshape(-1, features)
    gate_mat = w_gate[0]
    up_mat = w_up[0]
    down_mat = w_down[0]
    scale_row = hid_scale[0][None, :]
    pre_gate = jnp.dot(expert_rows, gate_mat, preferred_element_type=F32)
    pre_up = jnp.dot(expert_rows, up_mat, preferred_element_type=F32)
    sigmoid_val = jax.nn.sigmoid(pre_gate)
    activated = pre_gate * sigmoid_val
    hidden = (activated * pre_up * scale_row).astype(BF)
    scaled_grad = jnp.dot(expert_cot, down_mat.T, preferred_element_type=F32) * scale_row
    gate_delta = (
        scaled_grad * pre_up * sigmoid_val * (1.0 + pre_gate * (1.0 - sigmoid_val))
    ).astype(BF)
    up_delta = (scaled_grad * activated).astype(BF)
    contract_rows = (((0,), (0,)), ((), ()))
    down_grad = lax.dot_general(hidden, expert_cot, contract_rows, preferred_element_type=F32)
    gate_grad = lax.dot_general(expert_rows, gate_delta, contract_rows, preferred_element_type=F32)
    up_grad = lax.dot_general(expert_rows, up_delta, contract_rows, preferred_element_type=F32)
    part_out = jnp.dot(hidden, down_mat, preferred_element_type=F32).astype(BF)
    contract_hidden = (((1,), (1,)), ((), ()))
    part_grad = (
        lax.dot_general(gate_delta, gate_mat, contract_hidden, preferred_element_type=F32)
        + lax.dot_general(up_delta, up_mat, contract_hidden, preferred_element_type=F32)
    ).astype(BF)
    returned = give_back(jnp.stack([part_out, part_grad]).reshape(2, 32, 16, features))
    out_wide = returned[0].astype(F32)
    mixture = lax.dot_general(
        select_f * gate_value[:, None], out_wide, contract_rows, precision=HIGH
    )
    gate_pull = live * jnp.sum(picked_cot * out_wide, axis=-1)
    score_pick = gate_pull * raw_gate * (1.0 - raw_gate)
    by_row = select_f * score_pick[:, None]
    score_grad_t = jnp.sum(by_row.reshape(experts, slot_count, row_count), axis=1)
    token_grad = lax.dot_general(
        select_bf, returned[1], contract_rows, preferred_element_type=F32
    )
    token_grad = token_grad + lax.dot_general(
        score_grad_t, router.astype(F32).T, contract_rows, precision=HIGH
    )
    router_term = jnp.dot(score_grad_t, tokens.astype(F32), precision=HIGH)
    bias_term = jnp.sum(score_grad_t, axis=1)
    bias_tile = jnp.broadcast_to(
        jnp.pad(bias_term, (0, 512 - experts))[None, None, :], (8, 8, 512)
    )
    pieces = router_term.reshape(experts, 8, 512).transpose(1, 0, 2)
    reduced = reduce_all(jnp.concatenate([pieces, bias_tile], axis=1))
    quarter = lax.rem(lax.axis_index("exp"), 4)
    router_grad = lax.dynamic_slice(reduced, (0, quarter * 32), (experts, 32)).T
    threshold_grad = -reduced[16, :experts]
    return (
        mixture.astype(BF),
        token_grad.astype(BF),
        router_grad,
        threshold_grad,
        gate_grad[None],
        up_grad[None],
        down_grad[None],
    )


def solution(mesh):
    placed = (
        P(("seq", "exp"), None),
        P(("seq", "exp"), None),
        P(),
        P(),
        P("exp", None, "seq"),
        P("exp", None, "seq"),
        P("exp", "seq", None),
        P("exp", "seq"),
        P(("seq", "exp"), None, None),
        P(("seq", "exp"), None),
    )
    return jax.shard_map(
        on_device,
        mesh=mesh,
        in_specs=placed,
        out_specs=(
            P(("seq", "exp"), None),
            P(("seq", "exp"), None),
            P(("seq", "exp"), None),
            P(),
            P("exp", None, "seq"),
            P("exp", None, "seq"),
            P("exp", "seq", None),
        ),
        check_vma=False,
    )
```

time: 945 us -> 201 us (0.21); the launches traced: 934 us -> 199 us
  waiting for transfers between devices: 616 us -> 0 us
  blocking collectives: 174 us -> 0 us
  Pallas kernels: 0 us -> 139 us
  local copies, waits for them, and re-layouts: 48.3 us -> 11.1 us
  other arithmetic: 32.2 us -> 13.1 us
  between operations: 14.5 us -> 0.93 us
    unnamed x4 -> x0, waiting for transfers between devices: 551 us -> none
    pallas_call x0 -> x3, Pallas kernels: none -> 139 us  [the longest x1 64.2 us: dispatch(): pl.pallas_call(dispatch_kernel, out_shape=jax.ShapeDtypeStruct((2, 32, 16...]
    all_to_all x1 -> x0, blocking collectives: 107 us -> none  [on_device(): lax.all_to_all(copies, ('seq', 'exp'), split_axis=0, concat_axis=2, tiled...]
    psum x1 -> x0, blocking collectives: 67.3 us -> none  [on_device(): threshold_grad = -lax.psum(jnp.sum(score_grad, axis=0), ('seq', 'exp'))]
    reduce_scatter x2 -> x0, waiting for transfers between devices: 65.1 us -> none  [the longest x1 38.1 us: on_device(): lax.psum_scatter((first_term + lax.dot_general(up_delta, up_mat, contract...]
    scatter-add x3 -> x0, other arithmetic: 14.8 us -> none  [the longest x1 6 us: on_device(): token_grad = jnp.zeros((row_count, features), jnp.float32).at[flat_index]...]
    another operation x6 -> x0, local copies, waits for them, and re-layouts: 12.4 us -> none  [the longest x1 7.76 us: on_device(): copies = jnp.tile(stacked, (seq_count, 1, 1, 1))]
    convert_element_type x4 -> x0, other arithmetic: 10.7 us -> none  [the longest x1 3.84 us: on_device(): mixture.astype(jnp.bfloat16)]
  transfers between devices with their start and end apart: 4 -> 0, of which waited for: 3 -> 0; matrix products, arithmetic and copies ran while one was open for 6% -> 0% of each run, Pallas kernels for 0% -> 0%
where the time goes in v1:
time: 201 us; the launch traced here: 199 us
  Pallas kernels  139 us (69%)
  matrix products  35.5 us (18%)
  other arithmetic  13.1 us (7%)
  local copies, waits for them, and re-layouts  11.1 us (6%)
    pallas_call x1, Pallas kernels, dispatch(): pl.pallas_call(dispatch_kernel, out_shape=jax.ShapeDtypeStruct((2, 32, 16...  64.2 us
    pallas_call x1, Pallas kernels, give_back(): pl.pallas_call(return_kernel, out_shape=jax.ShapeDtypeStruct((2, 64, widt...  56.7 us
    pallas_call x1, Pallas kernels, reduce_all(): pl.pallas_call(reduce_kernel, out_shape=jax.ShapeDtypeStruct((24, 128), F...  17.8 us
    another operation x1, other arithmetic, on_device(): jnp.stack([part_out, part_grad]).reshape(2, 32, 16, features)  6.18 us
    slice x1, local copies, waits for them, and re-layouts, on_device(): expert_cot = arrived[1].reshape(-1, features)  4.07 us

profile of v1, /device:TPU:0, one launch (start us, length us, event | category | flops | bytes accessed | tf_op | source)
XLA Modules:
  0.0 199.2 jit_solution(16045982363515726379)
XLA Ops:
  0.6 2.4 %fusion.17 = f32[16,256]{1,0:T(8,128)S(1)} fusion(bf16[4096,16]{0,1:T(8,128)(2,1)} %param.12, bf16[256,4096]{1,0:T(8,128)(2,1)} %param.10, f32[16]{0:T(128)} %param.13), kind=kOutput, calls=%fused_computation.26 | convolution fusion | flops 33570816 | bytes 2244672 | tf_op jit(solution)/shard_map/dot_general | solution.py:375
  3.1 0.8 select_reduce_fusion.2
  4.8 0.8 copy.23
  5.6 1.7 multiply_convert_fusion
  7.4 1.3 convolution_convert_fusion.2.xr
  8.7 64.2 %shard_map.153 = bf16[2,32,16,4096]{3,2,1,0:T(8,128)(2,1)} custom-call(bf16[64,4096]{1,0:T(8,128)(2,1)} %convolution_convert_fusion.2.xr, bf16[64,4096]{1,0:T(8,128)(2,1)} %get-tuple-element.14.cr), custom_call_target="tpu_custom_call" | custom-call | tf_op jit(solution)/shard_map/pallas_call | solution.py:150
  73.0 4.1 %fusion.35 = (bf16[1,32,16,4096]{3,2,1,0:T(8,128)(2,1)S(1)}, bf16[1,32,16,4096]{3,2,1,0:T(8,128)(2,1)S(1)}) fusion(bf16[2,32,16,4096]{3,2,1,0:T(8,128)(2,1)} %shard_map.153), kind=kLoop, calls=%fused_computation.60 | loop fusion | bytes 16777216 | tf_op jit(solution)/shard_map/slice | solution.py:391
  77.1 1.6 fusion.9
  78.7 0.9 copy-done.12
  79.7 1.5 fusion.11
  81.4 1.6 multiply_convert_fusion.3
  83.1 1.3 fusion.7
  84.4 3.2 %add_convert_fusion = bf16[512,4096]{1,0:T(8,128)(2,1)} fusion(f32[512,4096]{1,0:T(8,128)S(1)} %fusion.7, bf16[512,192]{0,1:T(8,128)(2,1)S(1)} %get-tuple-element.13, bf16[1,4096,192]{1,2,0:T(8,128)(2,1)S(1)} %copy-done.11), kind=kOutput, calls=%fused_computation.1 | convolution fusion | flops 809500672 | bytes 14352384 | tf_op jit(solution)/shard_map/dot_general | solution.py:414
  87.6 1.3 convolution_convert_fusion
  88.9 6.2 %pad_maximum_fusion.p = bf16[2,32,16,4096]{3,2,1,0:T(8,128)(2,1)} fusion(bf16[1,32,16,4096]{3,2,1,0:T(8,128)(2,1)} %bitcast.77, bf16[1,32,16,4096]{3,2,1,0:T(8,128)(2,1)S(1)} %bitcast.75), kind=kLoop, calls=%fused_computation | loop fusion | flops 4194304 | bytes 16777216 | tf_op jit(solution)/shard_map/stack | solution.py:416
  95.1 56.7 %shard_map.154 = bf16[2,64,4096]{2,1,0:T(8,128)(2,1)} custom-call(bf16[2,32,16,4096]{3,2,1,0:T(8,128)(2,1)} %pad_maximum_fusion.p), custom_call_target="tpu_custom_call" | custom-call | tf_op jit(solution)/shard_map/pallas_call | solution.py:298
  151.8 1.2 multiply_reduce_fusion
  153.2 0.8 subtract_multiply_fusion
  154.0 1.4 select_reduce_fusion
  155.4 2.4 %copy.27 = bf16[4096,256]{1,0:T(8,128)(2,1)} copy(bf16[4096,256]{0,1:T(8,128)(2,1)S(1)} %bitcast.76) | data formatting | bytes 4194304 | tf_op jit(solution)/shard_map/dot_general | solution.py:431
  157.8 3.3 %convolution_bitcast_fusion.3 = f32[8,16,512]{2,1,0:T(8,128)S(1)} fusion(bf16[8,512,256]{2,1,0:T(8,128)(2,1)} %bitcast.78, f32[16,256]{1,0:T(8,128)S(1)} %get-tuple-element.8), kind=kOutput, calls=%fused_computation.21 | convolution fusion | flops 201326592 | bytes 2375680 | tf_op jit(solution)/shard_map/dot_general | solution.py:431
  161.2 0.7 pad.4
  161.9 0.8 pad_maximum_fusion.1.t
  162.7 17.8 %shard_map.155 = f32[24,128]{1,0:T(8,128)} custom-call(f32[8,24,512]{2,1,0:T(8,128)} %pad_maximum_fusion.1.t), custom_call_target="tpu_custom_call" | custom-call | tf_op jit(solution)/shard_map/pallas_call | solution.py:353
  180.4 1.4 dynamic-slice_bitcast_fusion
  181.8 1.2 negate_bitcast_fusion
  183.0 1.5 fusion.18
  184.5 3.4 %fusion = bf16[256,4096]{1,0:T(8,128)(2,1)} fusion(f32[256,4096]{1,0:T(8,128)S(1)} %fusion.18, f32[16,256]{1,0:T(8,128)S(1)} %get-tuple-element.8, bf16[4096,16]{0,1:T(8,128)(2,1)S(1)} %copy-done.15), kind=kOutput, calls=%fused_computation.4 | convolution fusion | flops 203423744 | bytes 6438912 | tf_op jit(solution)/shard_map/dot_general | solution.py:428
  187.9 3.2 %convolution_convert_fusion.1 = bf16[256,4096]{1,0:T(8,128)(2,1)} fusion(bf16[2,64,4096]{2,1,0:T(8,128)(2,1)S(1)} %copy-done.8, f32[64]{0:T(128)S(1)} %copy-done.19, s32[64]{0:T(128)S(1)} %copy-done.17), kind=kOutput, calls=%fused_computation.5 | convolution fusion | flops 806387712 | bytes 2622464 | tf_op jit(solution)/shard_map/dot_general | solution.py:418
  191.2 2.7 %convolution_bitcast_fusion = f32[1,4096,192]{1,2,0:T(8,128)} fusion(bf16[512,192]{0,1:T(8,128)(2,1)S(1)} %get-tuple-element.13, bf16[512,4096]{1,0:T(8,128)(2,1)S(1)} %bitcast.71), kind=kOutput, calls=%fused_computation.6 | convolution fusion | flops 805306368 | bytes 7536640 | tf_op jit(solution)/shard_map/dot_general | solution.py:409
  193.8 2.7 %convolution_bitcast_fusion.1 = f32[1,4096,192]{1,2,0:T(8,128)} fusion(bf16[512,192]{0,1:T(8,128)(2,1)S(1)} %copy-done.14, bf16[512,4096]{1,0:T(8,128)(2,1)S(1)} %bitcast.72), kind=kOutput, calls=%fused_computation.7 | convolution fusion | flops 805306368 | bytes 7536640 | tf_op jit(solution)/shard_map/dot_general | solution.py:408
  196.6 2.7 %convolution_bitcast_fusion.2 = f32[1,192,4096]{2,1,0:T(8,128)} fusion(bf16[512,192]{0,1:T(8,128)(2,1)S(1)} %get-tuple-element.11, bf16[512,4096]{1,0:T(8,128)(2,1)S(1)} %bitcast.74), kind=kOutput, calls=%fused_computation.8 | convolution fusion | flops 805306368 | bytes 7536640 | tf_op jit(solution)/shard_map/dot_general | solution.py:407
  (48 shorter events, 1.6 us)
Async XLA Ops:
  0.6 5.0 %copy-start = (bf16[256,4096]{1,0:T(8,128)(2,1)S(1)}, bf16[256,4096]{1,0:T(8,128)(2,1)}, u32[]{:S(2)}) copy-start(bf16[256,4096]{1,0:T(8,128)(2,1)} %param.11) | copy-start | bytes 6291460
  4.7 68.2 %copy-start.18 = (f32[64]{0:T(128)}, f32[64]{0:T(128)S(1)}, u32[]{:S(2)}) copy-start(f32[64]{0:T(128)S(1)} %mul.92) | copy-start | bytes 772
  5.6 67.3 %copy-start.16 = (s32[64]{0:T(128)}, s32[64]{0:T(128)S(1)}, u32[]{:S(2)}) copy-start(s32[64]{0:T(128)S(1)} %eq.25) | copy-start | bytes 772
  5.6 1.8 copy-start.6
  73.0 4.1 %copy-start.10 = (bf16[1,4096,192]{1,2,0:T(8,128)(2,1)S(1)}, bf16[1,4096,192]{1,2,0:T(8,128)(2,1)}, u32[]{:S(2)}) copy-start(bf16[1,4096,192]{1,2,0:T(8,128)(2,1)} %param.14) | copy-start | bytes 4718596
  77.0 4.2 %copy-start.2 = (bf16[1,32,16,4096]{3,2,1,0:T(8,128)(2,1)}, bf16[1,32,16,4096]{3,2,1,0:T(8,128)(2,1)S(1)}, u32[]{:S(2)}) copy-start(bf16[1,32,16,4096]{3,2,1,0:T(8,128)(2,1)S(1)} %get-tuple-element.10) | copy-start | bytes 12582916
  77.1 4.2 %copy-start.4 = (bf16[1,32,16,4096]{3,2,1,0:T(8,128)(2,1)}, bf16[1,32,16,4096]{3,2,1,0:T(8,128)(2,1)S(1)}, u32[]{:S(2)}) copy-start(bf16[1,32,16,4096]{3,2,1,0:T(8,128)(2,1)S(1)} %get-tuple-element.9) | copy-start | bytes 12582916
  77.1 2.6 %copy-start.12 = (bf16[1,192,4096]{2,1,0:T(8,128)(2,1)S(1)}, bf16[1,192,4096]{2,1,0:T(8,128)(2,1)}, u32[]{:S(2)}) copy-start(bf16[1,192,4096]{2,1,0:T(8,128)(2,1)} %param.16) | copy-start | bytes 4718596
  77.1 2.6 %copy-start.20 = (f32[1,192]{1,0:T(1,128)S(1)}, f32[1,192]{1,0:T(1,128)}, u32[]{:S(2)}) copy-start(f32[1,192]{1,0:T(1,128)} %param.17) | copy-start | bytes 2308
  78.7 2.7 %copy-start.11 = (bf16[1,4096,192]{1,2,0:T(8,128)(2,1)S(1)}, bf16[1,4096,192]{1,2,0:T(8,128)(2,1)}, u32[]{:S(2)}) copy-start(bf16[1,4096,192]{1,2,0:T(8,128)(2,1)} %param.15) | copy-start | bytes 4718596
  83.1 1.3 copy-start.13
  95.1 56.7 %copy-start.9 = (f32[64,4096]{1,0:T(8,128)S(1)}, f32[64,4096]{1,0:T(8,128)}, u32[]{:S(2)}) copy-start(f32[64,4096]{1,0:T(8,128)} %get-tuple-element.15) | copy-start | bytes 3145732
  95.1 60.3 %copy-start.7 = (bf16[256,4096]{1,0:T(8,128)(2,1)S(1)}, bf16[256,4096]{1,0:T(8,128)(2,1)}, u32[]{:S(2)}) copy-start(bf16[256,4096]{1,0:T(8,128)(2,1)} %param.10) | copy-start | bytes 6291460
  153.1 29.9 %copy-start.8 = (bf16[2,64,4096]{2,1,0:T(8,128)(2,1)S(1)}, bf16[2,64,4096]{2,1,0:T(8,128)(2,1)}, u32[]{:S(2)}) copy-start(bf16[2,64,4096]{2,1,0:T(8,128)(2,1)} %shard_map.154) | copy-start | bytes 3145732
  157.8 26.7 %copy-start.15 = (bf16[4096,16]{0,1:T(8,128)(2,1)S(1)}, bf16[4096,16]{0,1:T(8,128)(2,1)}, u32[]{:S(2)}) copy-start(bf16[4096,16]{0,1:T(8,128)(2,1)} %param.12) | copy-start | bytes 393220
  184.5 3.4 %copy-start.17 = (s32[64]{0:T(128)S(1)}, s32[64]{0:T(128)}, u32[]{:S(2)}) copy-start(s32[64]{0:T(128)} %copy-done.16) | copy-start | bytes 772
  184.5 3.4 %copy-start.19 = (f32[64]{0:T(128)S(1)}, f32[64]{0:T(128)}, u32[]{:S(2)}) copy-start(f32[64]{0:T(128)} %copy-done.18) | copy-start | bytes 772
  184.5 6.6 %copy-start.3 = (bf16[1,32,16,4096]{3,2,1,0:T(8,128)(2,1)S(1)}, bf16[1,32,16,4096]{3,2,1,0:T(8,128)(2,1)}, u32[]{:S(2)}) copy-start(bf16[1,32,16,4096]{3,2,1,0:T(8,128)(2,1)} %copy-done.2) | copy-start | bytes 12582916
  191.2 2.7 %copy-start.14 = (bf16[512,192]{0,1:T(8,128)(2,1)S(1)}, bf16[512,192]{0,1:T(8,128)(2,1)}, u32[]{:S(2)}) copy-start(bf16[512,192]{0,1:T(8,128)(2,1)} %copy-done.13) | copy-start | bytes 589828
  193.8 2.7 %copy-start.5 = (bf16[1,32,16,4096]{3,2,1,0:T(8,128)(2,1)S(1)}, bf16[1,32,16,4096]{3,2,1,0:T(8,128)(2,1)}, u32[]{:S(2)}) copy-start(bf16[1,32,16,4096]{3,2,1,0:T(8,128)(2,1)} %copy-done.4) | copy-start | bytes 12582916
  193.8 5.4 %copy-start.1 = (bf16[256,4096]{1,0:T(8,128)(2,1)S(1)}, bf16[256,4096]{1,0:T(8,128)(2,1)}, u32[]{:S(2)}) copy-start(bf16[256,4096]{1,0:T(8,128)(2,1)} %param.11) | copy-start | bytes 6291460

commit v2 on v0

v2 whole, which is shorter than its diff:
```python
import jax
import jax.numpy as jnp
from jax import lax
from jax.experimental import pallas as pl
from jax.experimental.pallas import tpu as pltpu
from jax.sharding import PartitionSpec as P

MESH = pl.DeviceIdType.MESH
BF = jnp.bfloat16
F32 = jnp.float32
HIGH = lax.Precision.HIGHEST
UP = (0, 2)
DOWN = (1, 3)


class Spot:
    def __init__(self):
        self.s = lax.axis_index("seq")
        self.e = lax.axis_index("exp")
        self.z = lax.div(self.s, 2)
        self.c = lax.rem(self.s, 2)
        self.y = lax.div(self.e, 4)
        self.x = lax.rem(self.e, 4)
        self.partner = (self.s + 1 - 2 * self.c, self.e)
        self.above = (self.layer(1) * 2 + self.c, self.e)
        self.below = (self.layer(3) * 2 + self.c, self.e)

    def layer(self, up):
        return lax.rem(self.z + up, 4)

    def group(self, i):
        return lax.rem(self.y + i, 4)

    def slot(self, up, other, i):
        core = self.c + other * (1 - 2 * self.c)
        return (self.layer(up) * 2 + core) * 4 + self.group(i)

    def in_plane(self, i, j):
        return lax.rem(self.y + i, 4) * 4 + lax.rem(self.x + j, 4)

    def plane_peers(self):
        return [(self.s, lax.rem(self.e + d, 16)) for d in range(1, 16)]

    def column_peers(self):
        return [(lax.rem(self.s + d, 8), self.e) for d in range(1, 8)]


def greet(peers):
    for peer in peers:
        pl.semaphore_signal(
            pltpu.get_barrier_semaphore(), inc=1, device_id=peer, device_id_type=MESH
        )


def greeted(count):
    pl.semaphore_wait(pltpu.get_barrier_semaphore(), count)


def push(src, dst, send_sem, recv_sem, device):
    copy = pltpu.make_async_remote_copy(
        src_ref=src,
        dst_ref=dst,
        send_sem=send_sem,
        recv_sem=recv_sem,
        device_id=device,
        device_id_type=MESH,
    )
    copy.start()
    return copy


def landed(dst, recv_sem, device):
    pltpu.make_async_remote_copy(
        src_ref=dst,
        dst_ref=dst,
        send_sem=recv_sem,
        recv_sem=recv_sem,
        device_id=device,
        device_id_type=MESH,
    ).wait_recv()


HOPS = [(i, j) for i in range(4) for j in (0, 1, 3, 2)]
NT = (((1,), (1,)), ((), ()))
TN = (((0,), (0,)), ((), ()))


def dot(a, b):
    return jnp.dot(a, b, preferred_element_type=F32)


def thirds(v):
    first = v.astype(BF)
    rest = v - first.astype(F32)
    second = rest.astype(BF)
    return first, second, (rest - second.astype(F32)).astype(BF)


def tiles(count, width, body):
    def step(j, carry):
        body(j, pl.ds(pl.multiple_of(j * width, width), width))
        return carry

    lax.fori_loop(0, count, step, 0)


def layer_kernel(
    tok_h, cot_h, wg_h, wu_h, wd_h, router, thr, scale, meta,
    mix_h, tgr_h, rows_h, red, hid, gdel, udel,
    tok, cot, wg, wu, wd, xr, cr, pc, msg, buf, xc, pp, pb, tot, xp, xm, om, rb, ret,
    pre_g, pre_u, hg, base, mix, tgr, t, ta, ext, tb,
    s1, r1, sp, rp, sm, rm, sq, rq, es, er, tps, tpr, tms, tmr, s3, r3, sa, ra, sb, rbs, loc,
):
    at = Spot()
    plane = at.plane_peers()
    column = at.column_peers()
    greet(plane + column)
    loads = [
        pltpu.make_async_copy(a, b, loc.at[k])
        for k, (a, b) in enumerate(
            [(tok_h, tok), (cot_h, cot), (wg_h, wg), (wu_h, wu), (wd_h, wd)]
        )
    ]
    for load in loads:
        load.start()

    pick = meta[:, 0:1]
    live = meta[:, 1:2].astype(F32)
    select = (pick == lax.broadcasted_iota(jnp.int32, (64, 256), 1)).astype(F32)
    select_bf = select.astype(BF)
    mine16 = (
        lax.div(lax.broadcasted_iota(jnp.int32, (64, 16), 0), 4)
        == lax.broadcasted_iota(jnp.int32, (64, 16), 1)
    ).astype(F32)
    loads[0].wait()
    gates = jax.nn.sigmoid(dot(tok[...], router[...]) - thr[...])
    chosen_gates = jnp.dot(select, gates, precision=HIGH, preferred_element_type=F32)
    raw = jnp.sum(chosen_gates * mine16, axis=1, keepdims=True)
    gate = raw * live

    def take_rows(j, cols):
        xr[:, cols] = dot(select_bf, tok[:, cols]).astype(BF)

    tiles(8, 512, take_rows)
    loads[1].wait()

    def take_cots(j, cols):
        cots = dot(select_bf, cot[:, cols])
        pc[:, cols] = cots.astype(BF)
        cr[:, cols] = (cots * gate).astype(BF)

    tiles(8, 512, take_cots)
    for e in range(16):
        msg[e, 0] = xr[4 * e : 4 * e + 4, :]
        msg[e, 1] = cr[4 * e : 4 * e + 4, :]
    greeted(22)

    sent = []
    own = pltpu.make_async_copy(msg.at[at.e], buf.at[at.e], loc.at[5])
    own.start()
    for i, j in HOPS:
        if i or j:
            e = at.in_plane(4 - i, j)
            k = i * 4 + j
            sent.append(push(msg.at[e], buf.at[at.e], s1.at[k], r1.at[k], (at.s, e)))
    own.wait()

    def hand_over(slot, q):
        sent.append(push(xc.at[:, slot], xc.at[:, slot], sq.at[q], rq.at[q], at.partner))

    def climb(slot, k):
        sent.append(push(xc.at[:, slot], xc.at[:, slot], sp.at[k], rp.at[k], at.above))

    def sink(slot, k):
        sent.append(push(xc.at[:, slot], xc.at[:, slot], sm.at[k], rm.at[k], at.below))

    for i in range(4):
        group = at.group(i)
        slot = at.slot(0, 0, i)
        for j in range(4):
            if i or j:
                landed(buf.at[at.in_plane(i, 4 - j)], r1.at[i * 4 + j], at.partner)
        for x in range(4):
            for a in range(2):
                xc[a, slot, 4 * x : 4 * x + 4, :] = buf[group * 4 + x, a]
        climb(slot, i)
        sink(slot, i)
        hand_over(slot, i)

    def from_beside(i):
        slot = at.slot(3, 0, i)
        landed(xc.at[:, slot], rp.at[i], at.above)
        if i in UP:
            climb(slot, 4 + UP.index(i))
        hand_over(slot, 4 + i)
        slot = at.slot(1, 0, i)
        landed(xc.at[:, slot], rm.at[i], at.below)
        if i in DOWN:
            sink(slot, 4 + DOWN.index(i))
        hand_over(slot, 8 + i)

    def from_across(i):
        slot = at.slot(2, 0, i)
        if i in UP:
            landed(xc.at[:, slot], rp.at[4 + UP.index(i)], at.above)
        else:
            landed(xc.at[:, slot], rm.at[4 + DOWN.index(i)], at.below)
        hand_over(slot, 12 + i)

    def from_partner(up):
        first = (0, 8, 12, 4)[up]
        for i in range(4):
            landed(xc.at[:, at.slot(up, 1, i)], rq.at[first + i], at.partner)

    def forward(up):
        lay = at.layer(up)
        slots = pl.ds(lay * 8, 8)
        pre_g[lay] = jnp.zeros_like(pre_g[lay])
        pre_u[lay] = jnp.zeros_like(pre_u[lay])

        def before(j, cols):
            a = xc[0, slots, :, cols].reshape(128, 1024)
            pre_g[lay] += dot(a, wg[cols, :])
            pre_u[lay] += dot(a, wu[cols, :])

        tiles(4, 1024, before)
        g = pre_g[lay]
        h = (g * jax.nn.sigmoid(g) * pre_u[lay] * scale[...]).astype(BF)
        hid[lay] = h

        def after(j, cols):
            pp[0, slots, :, cols] = dot(h, wd[:, cols]).astype(BF).reshape(8, 16, 512)

        tiles(8, 512, after)

    def backward(up):
        lay = at.layer(up)
        slots = pl.ds(lay * 8, 8)
        hg[...] = jnp.zeros_like(hg)

        def before(j, cols):
            a = xc[1, slots, :, cols].reshape(128, 1024)
            hg[...] += lax.dot_general(a, wd[:, cols], NT, preferred_element_type=F32)

        tiles(4, 1024, before)
        g = pre_g[lay]
        sig = jax.nn.sigmoid(g)
        grad = hg[...] * scale[...]
        gd = (grad * pre_u[lay] * sig * (1.0 + g * (1.0 - sig))).astype(BF)
        ud = (grad * (g * sig)).astype(BF)
        gdel[lay] = gd
        udel[lay] = ud

        def after(j, cols):
            v = lax.dot_general(gd, wg[cols, :], NT, preferred_element_type=F32)
            v = v + lax.dot_general(ud, wu[cols, :], NT, preferred_element_type=F32)
            pp[1, slots, :, cols] = v.astype(BF).reshape(8, 16, 512)

        tiles(8, 512, after)

    def trade(kind, up):
        slots = pl.ds(at.slot(up, 1, 0) - at.y, 4)
        sent.append(
            push(pp.at[kind, slots], pb.at[kind, up], es.at[kind, up], er.at[kind, up], at.partner)
        )

    def traded(kind, up):
        landed(pb.at[kind, up], er.at[kind, up], at.partner)

    def combine(kind, up, i, extra):
        q = up * 4 + i
        parts = [pp.at[kind, at.slot(up, 0, i)], pb.at[kind, up, at.group(i)]] + extra

        def add(j, cols):
            acc = parts[0][:, cols].astype(F32)
            for part in parts[1:]:
                acc = acc + part[:, cols].astype(F32)
            tot[kind, q, :, cols] = acc.astype(BF)

        tiles(4, 1024, add)
        return tot.at[kind, q]

    def up_send(kind, src, k):
        sent.append(push(src, xp.at[kind, k], tps.at[kind, k], tpr.at[kind, k], at.above))

    def down_send(kind, src, k):
        sent.append(push(src, xm.at[kind, k], tms.at[kind, k], tmr.at[kind, k], at.below))

    def from_below(kind, k):
        landed(xp.at[kind, k], tpr.at[kind, k], at.above)
        return xp.at[kind, k]

    def from_above(kind, k):
        landed(xm.at[kind, k], tmr.at[kind, k], at.below)
        return xm.at[kind, k]

    def send_plain(kind):
        for k in range(2):
            up_send(kind, combine(kind, 1, DOWN[k], []), k)
            down_send(kind, combine(kind, 3, UP[k], []), k)

    def send_across(kind):
        for k in range(2):
            up_send(kind, combine(kind, 2, UP[k], []), 2 + k)
            down_send(kind, combine(kind, 2, DOWN[k], []), 2 + k)

    def send_merged(kind):
        for k in range(2):
            up_send(kind, combine(kind, 1, UP[k], [from_below(kind, 2 + k)]), 4 + k)
            down_send(kind, combine(kind, 3, DOWN[k], [from_above(kind, 2 + k)]), 4 + k)

    def send_home(kind):
        for i in (1, 0, 3, 2):
            k = i // 2
            if i in UP:
                extra = [from_above(kind, k), from_below(kind, 4 + k)]
            else:
                extra = [from_below(kind, k), from_above(kind, 4 + k)]
            sums = combine(kind, 0, i, extra)
            for x in range(4):
                om[kind, i * 4 + x] = sums[4 * x : 4 * x + 4, :]
            for j in (1, 3, 2, 0):
                e = at.in_plane(i, j)
                src = om.at[kind, i * 4 + lax.rem(at.x + j, 4)]
                k = i * 4 + j
                if k:
                    sent.append(
                        push(src, rb.at[kind, at.e], s3.at[kind, k], r3.at[kind, k], (at.s, e))
                    )
                else:
                    pltpu.make_async_copy(src, rb.at[kind, at.e], loc.at[6 + kind]).start()

    def came_home(kind):
        for i, j in HOPS:
            e = at.in_plane(4 - i, 4 - j)
            if i or j:
                landed(rb.at[kind, e], r3.at[kind, i * 4 + j], at.partner)
            else:
                pltpu.make_async_copy(om.at[kind, at.x], rb.at[kind, e], loc.at[6 + kind]).wait()
        for e in range(16):
            ret[kind, 4 * e : 4 * e + 4, :] = rb[kind, e]

    for load in loads[2:]:
        load.wait()
    from_beside(0)
    from_partner(0)
    forward(0)
    from_beside(1)
    backward(0)
    trade(0, 0)
    trade(1, 0)
    from_beside(2)
    from_beside(3)
    from_partner(3)
    forward(3)
    trade(0, 3)
    from_partner(1)
    forward(1)
    trade(0, 1)
    from_across(0)
    from_across(1)
    traded(0, 3)
    traded(0, 1)
    send_plain(0)
    backward(3)
    trade(1, 3)
    backward(1)
    trade(1, 1)
    from_across(2)
    from_across(3)
    from_partner(2)
    forward(2)
    trade(0, 2)
    rows_out = pltpu.make_async_copy(xc, rows_h, loc.at[8])
    rows_out.start()
    traded(1, 3)
    traded(1, 1)
    traded(0, 2)
    send_across(0)
    send_plain(1)
    backward(2)
    trade(1, 2)
    send_merged(0)
    traded(1, 2)
    send_across(1)
    traded(0, 0)
    send_home(0)
    send_merged(1)
    came_home(0)

    pulls = jnp.zeros((64, 1), F32)
    for j in range(4):
        cols = slice(1024 * j, 1024 * j + 1024)
        pulls = pulls + jnp.sum(
            pc[:, cols].astype(F32) * ret[0, :, cols].astype(F32), axis=1, keepdims=True
        )
    score = live * pulls * raw * (1.0 - raw)
    by_row = select * score
    sgt = lax.dot_general(mine16, by_row, TN, precision=HIGH, preferred_element_type=F32)
    sg = lax.dot_general(by_row, mine16, TN, precision=HIGH, preferred_element_type=F32)
    parts = jnp.concatenate([v.astype(F32) for v in thirds(sgt)], axis=0).astype(BF)
    bias = jnp.broadcast_to(jnp.sum(sgt, axis=1, keepdims=True), (16, 512))

    def router_tile(j, cols):
        v = dot(parts, tok[:, cols])
        t[j, 0:16, :] = v[0:16] + v[16:32] + v[32:48]
        t[j, 16:32, :] = bias

    tiles(8, 512, router_tile)
    for d, peer in enumerate(column):
        sent.append(push(t.at[peer[0]], ta.at[d], sa.at[d], ra.at[d], peer))

    mix_parts = [w.T for w in (select * gate,)]
    w1, w2, w3 = thirds(mix_parts[0])
    sg1, sg2, sg3 = thirds(sg)

    def mix_tile(j, cols):
        rows = ret[0, :, cols]
        mix[:, cols] = (dot(w1, rows) + dot(w2, rows) + dot(w3, rows)).astype(BF)
        r = router[cols, :]
        v = lax.dot_general(sg1, r, NT, preferred_element_type=F32)
        v = v + lax.dot_general(sg2, r, NT, preferred_element_type=F32)
        base[:, cols] = v + lax.dot_general(sg3, r, NT, preferred_element_type=F32)

    tiles(8, 512, mix_tile)
    mix_out = pltpu.make_async_copy(mix, mix_h, loc.at[9])
    mix_out.start()

    acc = t[at.s]
    for d in range(7):
        landed(ta.at[d], ra.at[d], at.partner)
        acc = acc + ta[d]
    for y in range(4):
        ext[y, 0:16, :] = acc[0:16, 128 * y : 128 * y + 128]
        ext[y, 16:32, :] = acc[16:32, 0:128]
    for d, peer in enumerate(plane):
        sent.append(push(ext.at[lax.div(peer[1], 4)], tb.at[d], sb.at[d], rbs.at[d], peer))

    traded(1, 0)
    send_home(1)
    done = ext[at.y]
    for d in range(15):
        landed(tb.at[d], rbs.at[d], at.partner)
        done = done + tb[d]
    red[...] = done
    came_home(1)
    select_t = select.T.astype(BF)

    def grad_tile(j, cols):
        tgr[:, cols] = (base[:, cols] + dot(select_t, ret[1, :, cols])).astype(BF)

    tiles(8, 512, grad_tile)
    grad_out = pltpu.make_async_copy(tgr, tgr_h, loc.at[10])
    grad_out.start()
    for copy in sent:
        copy.wait_send()
    rows_out.wait()
    mix_out.wait()
    grad_out.wait()


def layer(tokens, cotangent, wg, wu, wd, router, thr, scale, meta):
    vmem = pl.BlockSpec(memory_space=pltpu.VMEM)
    hbm = pl.BlockSpec(memory_space=pl.ANY)
    dma = pltpu.SemaphoreType.DMA
    v = pltpu.VMEM
    width = tokens.shape[1]
    units = wg.shape[1]
    shape = jax.ShapeDtypeStruct
    return pl.pallas_call(
        layer_kernel,
        out_shape=(
            shape((256, width), BF),
            shape((256, width), BF),
            shape((2, 32, 16, width), BF),
            shape((32, 128), F32),
            shape((4, 128, units), BF),
            shape((4, 128, units), BF),
            shape((4, 128, units), BF),
        ),
        in_specs=[hbm] * 5 + [vmem] * 4,
        out_specs=(hbm, hbm, hbm, vmem, vmem, vmem, vmem),
        scratch_shapes=[
            v((256, width), BF), v((256, width), BF),
            v((width, units), BF), v((width, units), BF), v((units, width), BF),
            v((64, width), BF), v((64, width), BF), v((64, width), BF),
            v((16, 2, 4, width), BF), v((16, 2, 4, width), BF),
            v((2, 32, 16, width), BF), v((2, 32, 16, width), BF),
            v((2, 4, 4, 16, width), BF), v((2, 16, 16, width), BF),
            v((2, 6, 16, width), BF), v((2, 6, 16, width), BF),
            v((2, 16, 4, width), BF), v((2, 16, 4, width), BF), v((2, 64, width), BF),
            v((4, 128, units), F32), v((4, 128, units), F32), v((128, units), F32),
            v((256, width), F32), v((256, width), BF), v((256, width), BF),
            v((8, 32, 512), F32), v((7, 32, 512), F32), v((4, 32, 128), F32),
            v((15, 32, 128), F32),
            dma((16,)), dma((16,)), dma((6,)), dma((6,)), dma((6,)), dma((6,)),
            dma((16,)), dma((16,)), dma((2, 4)), dma((2, 4)),
            dma((2, 6)), dma((2, 6)), dma((2, 6)), dma((2, 6)),
            dma((2, 16)), dma((2, 16)), dma((7,)), dma((7,)), dma((15,)), dma((15,)),
            dma((11,)),
        ],
        compiler_params=pltpu.CompilerParams(
            collective_id=0, has_side_effects=True, vmem_limit_bytes=67043328
        ),
    )(tokens, cotangent, wg, wu, wd, router, thr, scale, meta)


def on_device(tokens, cotangent, router, threshold, w_gate, w_up, w_down, hid_scale, picks, counts):
    experts = router.shape[1]
    slot_count = picks.shape[2]
    features = tokens.shape[1]
    active = jnp.arange(slot_count, dtype=jnp.int32)[None, :] < counts[0][:, None]
    meta = jnp.stack([picks[0], active.astype(jnp.int32)], axis=-1).reshape(-1, 2)
    mixture, token_grad, rows, reduced, hidden, gate_delta, up_delta = layer(
        tokens, cotangent, w_gate[0], w_up[0], w_down[0], router,
        threshold[None, :], hid_scale[0][None, :], meta,
    )
    expert_rows = rows[0].reshape(-1, features)
    expert_cot = rows[1].reshape(-1, features)
    flat = (expert_rows.shape[0], -1)
    down_grad = lax.dot_general(
        hidden.reshape(flat), expert_cot, TN, preferred_element_type=F32
    )
    gate_grad = lax.dot_general(
        expert_rows, gate_delta.reshape(flat), TN, preferred_element_type=F32
    )
    up_grad = lax.dot_general(
        expert_rows, up_delta.reshape(flat), TN, preferred_element_type=F32
    )
    quarter = lax.rem(lax.axis_index("exp"), 4)
    router_grad = lax.dynamic_slice(reduced, (0, quarter * 32), (experts, 32)).T
    threshold_grad = -reduced[experts : 2 * experts, 0]
    return (
        mixture,
        token_grad,
        router_grad,
        threshold_grad,
        gate_grad[None],
        up_grad[None],
        down_grad[None],
    )


def solution(mesh):
    placed = (
        P(("seq", "exp"), None),
        P(("seq", "exp"), None),
        P(),
        P(),
        P("exp", None, "seq"),
        P("exp", None, "seq"),
        P("exp", "seq", None),
        P("exp", "seq"),
        P(("seq", "exp"), None, None),
        P(("seq", "exp"), None),
    )
    return jax.shard_map(
        on_device,
        mesh=mesh,
        in_specs=placed,
        out_specs=(
            P(("seq", "exp"), None),
            P(("seq", "exp"), None),
            P(("seq", "exp"), None),
            P(),
            P("exp", None, "seq"),
            P("exp", None, "seq"),
            P("exp", "seq", None),
        ),
        check_vma=False,
    )
```

time: 945 us -> 151 us (0.16); the launches traced: 934 us -> 150 us
  waiting for transfers between devices: 616 us -> 0 us
  blocking collectives: 174 us -> 0 us
  Pallas kernels: 0 us -> 120 us
  matrix products: 41.6 us -> 8.15 us
  other arithmetic: 32.2 us -> 1.34 us
  local copies, waits for them, and re-layouts: 48.3 us -> 20.1 us
  between operations: 14.5 us -> 0.72 us
    unnamed x4 -> x0, waiting for transfers between devices: 551 us -> none
    pallas_call x0 -> x1, Pallas kernels: none -> 120 us  [layer(): pl.pallas_call(layer_kernel, out_shape=(shape((256, width), BF), shape((2...]
    all_to_all x1 -> x0, blocking collectives: 107 us -> none  [on_device(): lax.all_to_all(copies, ('seq', 'exp'), split_axis=0, concat_axis=2, tiled...]
    psum x1 -> x0, blocking collectives: 67.3 us -> none  [on_device(): threshold_grad = -lax.psum(jnp.sum(score_grad, axis=0), ('seq', 'exp'))]
    reduce_scatter x2 -> x0, waiting for transfers between devices: 65.1 us -> none  [the longest x1 38.1 us: on_device(): lax.psum_scatter((first_term + lax.dot_general(up_delta, up_mat, contract...]
    dot_general x12 -> x3, matrix products: 41.6 us -> 8.15 us  [the longest x1 2.73 us: on_device(): lax.dot_general(expert_rows, up_delta.reshape(flat), TN, preferred_elemen...]
    scatter-add x3 -> x0, other arithmetic: 14.8 us -> none  [the longest x1 6 us: on_device(): token_grad = jnp.zeros((row_count, features), jnp.float32).at[flat_index]...]
    another operation x6 -> x2, local copies, waits for them, and re-layouts: 12.4 us -> 0.8 us  [on_device(): jnp.stack([picks[0], active.astype(jnp.int32)], axis=-1).reshape(-1, 2)]
  transfers between devices with their start and end apart: 4 -> 0, of which waited for: 3 -> 0; matrix products, arithmetic and copies ran while one was open for 6% -> 0% of each run, Pallas kernels for 0% -> 0%
where the time goes in v2:
time: 151 us; the launch traced here: 150 us
  Pallas kernels  120 us (79%)
  local copies, waits for them, and re-layouts  20.1 us (13%)
  matrix products  8.15 us (5%)
    pallas_call x1, Pallas kernels, layer(): pl.pallas_call(layer_kernel, out_shape=(shape((256, width), BF), shape((2...  120 us
    unnamed x18, local copies, waits for them, and re-layouts  13 us
    slice x1, local copies, waits for them, and re-layouts, on_device(): expert_cot = rows[1].reshape(-1, features)  3.99 us

profile of v2, /device:TPU:0, one launch (start us, length us, event | category | flops | bytes accessed | tf_op | source)
XLA Modules:
  0.0 150.0 jit_solution(13601636767048997792)
XLA Ops:
  0.6 0.0 copy-start.2
  0.7 0.9 copy.33
  1.5 0.1 stack.6
  1.6 0.7 lt.33
  2.3 0.1 lt.34
  2.4 0.1 lt.31
  2.6 0.7 copy.35.meta
  3.3 2.2 %copy.34.router = bf16[4096,16]{1,0:T(8,128)(2,1)} copy(bf16[4096,16]{0,1:T(8,128)(2,1)} %param.12) | data formatting | bytes 262144 | tf_op args[2]
  5.5 3.8 %copy.31 = bf16[1,4096,192]{2,1,0:T(8,128)(2,1)} copy(bf16[1,4096,192]{1,2,0:T(8,128)(2,1)} %param.14) | data formatting | bytes 3145728 | tf_op args[4]
  9.3 0.0 copy-done.2
  9.3 2.4 %copy.32 = bf16[1,4096,192]{2,1,0:T(8,128)(2,1)} copy(bf16[1,4096,192]{1,2,0:T(8,128)(2,1)S(1)} %copy-done.2) | data formatting | bytes 3145728 | tf_op args[5]
  11.7 119.8 %shard_map.153 = (bf16[256,4096]{1,0:T(8,128)(2,1)}, bf16[256,4096]{1,0:T(8,128)(2,1)}, bf16[2,32,16,4096]{3,2,1,0:T(8,128)(2,1)}, f32[32,128]{1,0:T(8,128)}, bf...) custom-call(bf16[256,4096]{1,0:T(8,128)(2,1)} %tok_h.1, ...), custom_call_target="tpu_custom_call" | custom-call | tf_op jit(solution)/shard_map/pallas_call | solution.py:470
  131.5 1.3 negate_reduce_fusion
  132.8 1.4 dynamic-slice_bitcast_fusion
  134.2 0.0 copy-start.3
  134.2 4.0 %fusion = (bf16[1,32,16,4096]{3,2,1,0:T(8,128)(2,1)S(1)}, bf16[1,32,16,4096]{3,2,1,0:T(8,128)(2,1)S(1)}) fusion(bf16[2,32,16,4096]{3,2,1,0:T(8,128)(2,1)} %get-tuple-element.17), kind=kLoop, calls=%fused_computation.7 | loop fusion | bytes 16777216 | tf_op jit(solution)/shard_map/slice | solution.py:519
  138.2 0.0 copy-done.3
  138.2 0.0 copy-start.5
  138.2 2.7 %convolution_bitcast_fusion = f32[1,192,4096]{2,1,0:T(8,128)} fusion(bf16[512,192]{1,0:T(8,128)(2,1)S(1)} %bitcast.34, bf16[512,4096]{1,0:T(8,128)(2,1)S(1)} %bitcast.30), kind=kOutput, calls=%fused_computation | convolution fusion | flops 805306368 | bytes 7536640 | tf_op jit(solution)/shard_map/dot_general | solution.py:521
  140.9 0.0 copy-done.5
  140.9 0.0 copy-start.4
  140.9 2.7 %convolution_bitcast_fusion.1 = f32[1,4096,192]{1,2,0:T(8,128)} fusion(bf16[512,4096]{1,0:T(8,128)(2,1)S(1)} %bitcast.28, bf16[512,192]{1,0:T(8,128)(2,1)S(1)} %bitcast.36), kind=kOutput, calls=%fused_computation.1 | convolution fusion | flops 805306368 | bytes 7536640 | tf_op jit(solution)/shard_map/dot_general | solution.py:527
  143.6 0.0 copy-done.4
  143.6 0.0 copy-start.1
  143.6 2.7 %convolution_bitcast_fusion.2 = f32[1,4096,192]{1,2,0:T(8,128)} fusion(bf16[512,4096]{1,0:T(8,128)(2,1)S(1)} %bitcast.29, bf16[512,192]{1,0:T(8,128)(2,1)S(1)} %bitcast.35), kind=kOutput, calls=%fused_computation.2 | convolution fusion | flops 805306368 | bytes 7536640 | tf_op jit(solution)/shard_map/dot_general | solution.py:524
  146.4 0.0 copy-done.1
  146.4 0.0 copy-start
  146.4 1.3 copy.38
  147.7 1.0 copy-done
  148.7 1.3 copy.39
  (3 shorter events, 0.0 us)
Async XLA Ops:
  0.6 8.7 %copy-start.2 = (bf16[1,4096,192]{1,2,0:T(8,128)(2,1)S(1)}, bf16[1,4096,192]{1,2,0:T(8,128)(2,1)}, u32[]{:S(2)}) copy-start(bf16[1,4096,192]{1,2,0:T(8,128)(2,1)} %param.15) | copy-start | bytes 4718596
  134.2 4.0 %copy-start.3 = (bf16[4,128,192]{2,1,0:T(8,128)(2,1)S(1)}, bf16[4,128,192]{2,1,0:T(8,128)(2,1)}, u32[]{:S(2)}) copy-start(bf16[4,128,192]{2,1,0:T(8,128)(2,1)} %get-tuple-element.20) | copy-start | bytes 589828
  138.2 2.7 %copy-start.5 = (bf16[4,128,192]{2,1,0:T(8,128)(2,1)S(1)}, bf16[4,128,192]{2,1,0:T(8,128)(2,1)}, u32[]{:S(2)}) copy-start(bf16[4,128,192]{2,1,0:T(8,128)(2,1)} %get-tuple-element.19) | copy-start | bytes 589828
  140.9 2.7 %copy-start.4 = (bf16[4,128,192]{2,1,0:T(8,128)(2,1)S(1)}, bf16[4,128,192]{2,1,0:T(8,128)(2,1)}, u32[]{:S(2)}) copy-start(bf16[4,128,192]{2,1,0:T(8,128)(2,1)} %get-tuple-element.18) | copy-start | bytes 589828
  143.6 2.7 %copy-start.1 = (bf16[256,4096]{1,0:T(8,128)(2,1)S(1)}, bf16[256,4096]{1,0:T(8,128)(2,1)}, u32[]{:S(2)}) copy-start(bf16[256,4096]{1,0:T(8,128)(2,1)} %get-tuple-element.30) | copy-start | bytes 6291460
  146.4 2.3 %copy-start = (bf16[256,4096]{1,0:T(8,128)(2,1)S(1)}, bf16[256,4096]{1,0:T(8,128)(2,1)}, u32[]{:S(2)}) copy-start(bf16[256,4096]{1,0:T(8,128)(2,1)} %get-tuple-element.31) | copy-start | bytes 6291460

commit v3 on v2

v3 whole, which is shorter than its diff:
```python
import jax
import jax.numpy as jnp
from jax import lax
from jax.experimental import pallas as pl
from jax.experimental.pallas import tpu as pltpu
from jax.sharding import PartitionSpec as P

MESH = pl.DeviceIdType.MESH
BF = jnp.bfloat16
F32 = jnp.float32
HIGH = lax.Precision.HIGHEST
UP = (0, 2)
DOWN = (1, 3)


class Spot:
    def __init__(self):
        self.s = lax.axis_index("seq")
        self.e = lax.axis_index("exp")
        self.z = lax.div(self.s, 2)
        self.c = lax.rem(self.s, 2)
        self.y = lax.div(self.e, 4)
        self.x = lax.rem(self.e, 4)
        self.partner = (self.s + 1 - 2 * self.c, self.e)
        self.above = (self.layer(1) * 2 + self.c, self.e)
        self.below = (self.layer(3) * 2 + self.c, self.e)

    def layer(self, up):
        return lax.rem(self.z + up, 4)

    def group(self, i):
        return lax.rem(self.y + i, 4)

    def slot(self, up, other, i):
        core = self.c + other * (1 - 2 * self.c)
        return (self.layer(up) * 2 + core) * 4 + self.group(i)

    def in_plane(self, i, j):
        return lax.rem(self.y + i, 4) * 4 + lax.rem(self.x + j, 4)

    def at_layer(self, up):
        return (self.layer(up) * 2 + self.c, self.e)

    def plane_peers(self):
        return [(self.s, lax.rem(self.e + d, 16)) for d in range(1, 16)]

    def column_peers(self):
        return [(lax.rem(self.s + d, 8), self.e) for d in range(1, 8)]


def greet(peers):
    for peer in peers:
        pl.semaphore_signal(
            pltpu.get_barrier_semaphore(), inc=1, device_id=peer, device_id_type=MESH
        )


def greeted(count):
    pl.semaphore_wait(pltpu.get_barrier_semaphore(), count)


def push(src, dst, send_sem, recv_sem, device):
    copy = pltpu.make_async_remote_copy(
        src_ref=src,
        dst_ref=dst,
        send_sem=send_sem,
        recv_sem=recv_sem,
        device_id=device,
        device_id_type=MESH,
    )
    copy.start()
    return copy


def landed(dst, recv_sem, device):
    pltpu.make_async_remote_copy(
        src_ref=dst,
        dst_ref=dst,
        send_sem=recv_sem,
        recv_sem=recv_sem,
        device_id=device,
        device_id_type=MESH,
    ).wait_recv()


HOPS = [(i, j) for i in range(4) for j in (0, 1, 3, 2)]
NT = (((1,), (1,)), ((), ()))
TN = (((0,), (0,)), ((), ()))


def dot(a, b):
    return jnp.dot(a, b, preferred_element_type=F32)


def thirds(v):
    first = v.astype(BF)
    rest = v - first.astype(F32)
    second = rest.astype(BF)
    return first, second, (rest - second.astype(F32)).astype(BF)


def tiles(count, width, body):
    def step(j, carry):
        body(j, pl.ds(pl.multiple_of(j * width, width), width))
        return carry

    lax.fori_loop(0, count, step, 0)


def layer_kernel(
    tok_h, cot_h, wg_h, wu_h, wd_h, router, thr, scale, picks, counts,
    mix_h, tgr_h, gate_h, up_h, down_h, red, thr_out,
    tok, cot, wg, wu, wd, xr, cr, pc, msg, buf, xc, pp, pb, tot, xp, xm, om, rb, ret,
    pre_g, pre_u, hg, hid_t, del_t, wgr, base, mix, tgr, t, ta, tz, tzr, ext, tb,
    s1, r1, sp, rp, sm, rm, sq, rq, es, er, tps, tpr, tms, tmr, s3, r3,
    pas, par, zs, zr, sb, rbs, loc,
):
    at = Spot()
    plane = at.plane_peers()
    column = at.column_peers()
    greet(plane + column)
    loads = [
        pltpu.make_async_copy(a, b, loc.at[k])
        for k, (a, b) in enumerate(
            [(tok_h, tok), (cot_h, cot), (wg_h, wg), (wu_h, wu), (wd_h, wd)]
        )
    ]
    loads[0].start()

    row = lax.broadcasted_iota(jnp.int32, (64, 16), 0)
    lane = lax.broadcasted_iota(jnp.int32, (64, 16), 1)
    mine16 = (lax.div(row, 4) == lane).astype(F32)
    turn = lax.rem(row, 4)
    listed = picks[...].astype(F32)
    wide = jnp.zeros((64, 16), F32)
    for k in range(4):
        wide = jnp.where(turn == k, listed[k : k + 1, :], wide)
    pick = jnp.sum(wide * mine16, axis=1, keepdims=True)
    limit = jnp.sum(mine16 * counts[...].astype(F32), axis=1, keepdims=True)
    live = (turn[:, 0:1].astype(F32) < limit).astype(F32)
    select = (
        pick == lax.broadcasted_iota(jnp.int32, (64, 256), 1).astype(F32)
    ).astype(F32)
    select_bf = select.astype(BF)
    loads[0].wait()
    loads[1].start()

    def take_rows(j, cols):
        xr[:, cols] = dot(select_bf, tok[:, cols]).astype(BF)

    tiles(8, 512, take_rows)
    for e in range(16):
        msg[0, e] = xr[4 * e : 4 * e + 4, :]
    greeted(22)

    sent = []

    def scatter(kind):
        mine = pltpu.make_async_copy(msg.at[kind, at.e], buf.at[kind, at.e], loc.at[5 + kind])
        mine.start()
        for i, j in HOPS:
            if i or j:
                e = at.in_plane(4 - i, j)
                k = i * 4 + j
                sent.append(
                    push(
                        msg.at[kind, e], buf.at[kind, at.e], s1.at[kind, k], r1.at[kind, k],
                        (at.s, e),
                    )
                )
        mine.wait()

    scatter(0)
    gates = jax.nn.sigmoid(
        lax.dot_general(tok[...], router[...], NT, preferred_element_type=F32) - thr[...]
    )
    chosen_gates = jnp.dot(select, gates, precision=HIGH, preferred_element_type=F32)
    raw = jnp.sum(chosen_gates * mine16, axis=1, keepdims=True)
    gate = raw * live
    loads[1].wait()
    for load in loads[2:]:
        load.start()

    def take_cots(j, cols):
        cots = dot(select_bf, cot[:, cols])
        pc[:, cols] = cots.astype(BF)
        cr[:, cols] = (cots * gate).astype(BF)

    tiles(8, 512, take_cots)
    for e in range(16):
        msg[1, e] = cr[4 * e : 4 * e + 4, :]
    scatter(1)

    def hand_over(kind, slot, q):
        ref = xc.at[kind, slot]
        sent.append(push(ref, ref, sq.at[kind, q], rq.at[kind, q], at.partner))

    def climb(kind, slot, k):
        ref = xc.at[kind, slot]
        sent.append(push(ref, ref, sp.at[kind, k], rp.at[kind, k], at.above))

    def sink(kind, slot, k):
        ref = xc.at[kind, slot]
        sent.append(push(ref, ref, sm.at[kind, k], rm.at[kind, k], at.below))

    def gather(kind, i):
        group = at.group(i)
        slot = at.slot(0, 0, i)
        for j in range(4):
            if i or j:
                landed(buf.at[kind, at.in_plane(i, 4 - j)], r1.at[kind, i * 4 + j], at.partner)
        for x in range(4):
            xc[kind, slot, 4 * x : 4 * x + 4, :] = buf[kind, group * 4 + x]
        climb(kind, slot, i)
        sink(kind, slot, i)
        hand_over(kind, slot, i)

    def from_beside(kind, i):
        slot = at.slot(3, 0, i)
        landed(xc.at[kind, slot], rp.at[kind, i], at.above)
        if i in UP:
            climb(kind, slot, 4 + UP.index(i))
        hand_over(kind, slot, 4 + i)
        slot = at.slot(1, 0, i)
        landed(xc.at[kind, slot], rm.at[kind, i], at.below)
        if i in DOWN:
            sink(kind, slot, 4 + DOWN.index(i))
        hand_over(kind, slot, 8 + i)

    def from_across(kind, i):
        slot = at.slot(2, 0, i)
        if i in UP:
            landed(xc.at[kind, slot], rp.at[kind, 4 + UP.index(i)], at.above)
        else:
            landed(xc.at[kind, slot], rm.at[kind, 4 + DOWN.index(i)], at.below)
        hand_over(kind, slot, 12 + i)

    def from_partner(kind, up):
        first = (0, 8, 12, 4)[up]
        for i in range(4):
            landed(xc.at[kind, at.slot(up, 1, i)], rq.at[kind, first + i], at.partner)

    def stacked(kind, lays, cols, width):
        parts = [xc[kind, pl.ds(lay * 8, 8), :, cols].reshape(128, width) for lay in lays]
        return parts[0] if len(parts) == 1 else jnp.concatenate(parts, axis=0)

    def spread(kind, lays, cols, v):
        for n, lay in enumerate(lays):
            piece = v[128 * n : 128 * n + 128]
            pp[kind, pl.ds(lay * 8, 8), :, cols] = piece.astype(BF).reshape(8, 16, 512)

    def keep_t(ref, first, lays, v):
        for n, lay in enumerate(lays):
            cols = pl.ds(pl.multiple_of(lay * 128, 128), 128)
            ref[first : first + 192, cols] = v[128 * n : 128 * n + 128].T.astype(BF)

    def forward(*ups):
        lays = [at.layer(up) for up in ups]
        rows = 128 * len(ups)
        low = {1: 0, 2: 256, 0: 384}[ups[0]]
        span = slice(low, low + rows)
        pre_g[span] = jnp.zeros((rows, 192), F32)
        pre_u[span] = jnp.zeros((rows, 192), F32)

        def before(j, cols):
            a = stacked(0, lays, cols, 1024)
            pre_g[span] += lax.dot_general(a, wg[:, cols], NT, preferred_element_type=F32)
            pre_u[span] += lax.dot_general(a, wu[:, cols], NT, preferred_element_type=F32)

        tiles(4, 1024, before)
        g = pre_g[span]
        hidden = g * jax.nn.sigmoid(g) * pre_u[span] * scale[...]
        h = hidden.astype(BF)
        keep_t(hid_t, 0, lays, hidden)

        def after(j, cols):
            spread(0, lays, cols, dot(h, wd[:, cols]))

        tiles(8, 512, after)

    def backward(*ups):
        lays = [at.layer(up) for up in ups]
        rows = 128 * len(ups)
        low = {1: 0, 2: 256, 0: 384}[ups[0]]
        span = slice(low, low + rows)
        hg[0:rows] = jnp.zeros((rows, 192), F32)

        def before(j, cols):
            a = stacked(1, lays, cols, 1024)
            hg[0:rows] += lax.dot_general(a, wd[:, cols], NT, preferred_element_type=F32)

        tiles(4, 1024, before)
        g = pre_g[span]
        sig = jax.nn.sigmoid(g)
        grad = hg[0:rows] * scale[...]
        gate_delta = grad * pre_u[span] * sig * (1.0 + g * (1.0 - sig))
        up_delta = grad * (g * sig)
        gd = gate_delta.astype(BF)
        ud = up_delta.astype(BF)
        keep_t(del_t, 0, lays, gate_delta)
        keep_t(del_t, 192, lays, up_delta)

        def after(j, cols):
            spread(1, lays, cols, dot(gd, wg[:, cols]) + dot(ud, wu[:, cols]))

        tiles(8, 512, after)

    def trade(kind, up):
        slots = pl.ds(at.slot(up, 1, 0) - at.y, 4)
        sent.append(
            push(pp.at[kind, slots], pb.at[kind, up], es.at[kind, up], er.at[kind, up], at.partner)
        )

    def traded(kind, up):
        landed(pb.at[kind, up], er.at[kind, up], at.partner)

    def combine(kind, up, i, extra):
        q = up * 4 + i
        parts = [pp.at[kind, at.slot(up, 0, i)], pb.at[kind, up, at.group(i)]] + extra

        def add(j, cols):
            acc = parts[0][:, cols].astype(F32)
            for part in parts[1:]:
                acc = acc + part[:, cols].astype(F32)
            tot[kind, q, :, cols] = acc.astype(BF)

        tiles(4, 1024, add)
        return tot.at[kind, q]

    def up_send(kind, src, k):
        sent.append(push(src, xp.at[kind, k], tps.at[kind, k], tpr.at[kind, k], at.above))

    def down_send(kind, src, k):
        sent.append(push(src, xm.at[kind, k], tms.at[kind, k], tmr.at[kind, k], at.below))

    def from_below(kind, k):
        landed(xp.at[kind, k], tpr.at[kind, k], at.above)
        return xp.at[kind, k]

    def from_above(kind, k):
        landed(xm.at[kind, k], tmr.at[kind, k], at.below)
        return xm.at[kind, k]

    def send_plain(kind):
        for k in range(2):
            up_send(kind, combine(kind, 1, DOWN[k], []), k)
            down_send(kind, combine(kind, 3, UP[k], []), k)

    def send_across(kind):
        for k in range(2):
            up_send(kind, combine(kind, 2, UP[k], []), 2 + k)
            down_send(kind, combine(kind, 2, DOWN[k], []), 2 + k)

    def send_merged(kind):
        for k in range(2):
            up_send(kind, combine(kind, 1, UP[k], [from_below(kind, 2 + k)]), 4 + k)
            down_send(kind, combine(kind, 3, DOWN[k], [from_above(kind, 2 + k)]), 4 + k)

    def send_home(kind):
        for i in (1, 0, 3, 2):
            k = i // 2
            if i in UP:
                extra = [from_above(kind, k), from_below(kind, 4 + k)]
            else:
                extra = [from_below(kind, k), from_above(kind, 4 + k)]
            sums = combine(kind, 0, i, extra)
            for x in range(4):
                om[kind, i * 4 + x] = sums[4 * x : 4 * x + 4, :]
            for j in (1, 3, 2, 0):
                e = at.in_plane(i, j)
                src = om.at[kind, i * 4 + lax.rem(at.x + j, 4)]
                k = i * 4 + j
                if k:
                    sent.append(
                        push(src, rb.at[kind, at.e], s3.at[kind, k], r3.at[kind, k], (at.s, e))
                    )
                else:
                    pltpu.make_async_copy(src, rb.at[kind, at.e], loc.at[7 + kind]).start()

    def came_home(kind):
        for i, j in HOPS:
            e = at.in_plane(4 - i, 4 - j)
            if i or j:
                landed(rb.at[kind, e], r3.at[kind, i * 4 + j], at.partner)
            else:
                pltpu.make_async_copy(om.at[kind, at.x], rb.at[kind, e], loc.at[7 + kind]).wait()
        for e in range(16):
            ret[kind, 4 * e : 4 * e + 4, :] = rb[kind, e]

    for i in range(4):
        gather(0, i)
    from_beside(0, 0)
    gather(1, 0)
    gather(1, 1)
    from_beside(0, 1)
    gather(1, 2)
    gather(1, 3)
    from_partner(0, 0)
    for load in loads[2:]:
        load.wait()
    forward(0)
    trade(0, 0)
    from_beside(0, 2)
    from_beside(0, 3)
    from_across(0, 0)
    from_across(0, 1)
    from_partner(0, 3)
    from_partner(0, 1)
    forward(1, 3)
    trade(0, 1)
    trade(0, 3)
    from_beside(1, 0)
    from_beside(1, 1)
    from_across(0, 2)
    from_across(0, 3)
    traded(0, 1)
    traded(0, 3)
    send_plain(0)
    from_partner(0, 2)
    forward(2)
    trade(0, 2)
    from_beside(1, 2)
    from_beside(1, 3)
    from_partner(1, 0)
    traded(0, 2)
    send_across(0)
    from_across(1, 0)
    from_across(1, 1)
    backward(0)
    trade(1, 0)
    from_across(1, 2)
    from_across(1, 3)
    from_partner(1, 3)
    from_partner(1, 1)
    backward(1, 3)
    trade(1, 1)
    trade(1, 3)
    send_merged(0)
    from_partner(1, 2)
    traded(1, 1)
    traded(1, 3)
    send_plain(1)
    backward(2)
    trade(1, 2)
    traded(1, 2)
    send_across(1)

    def weight_tile(j, cols):
        v = dot(del_t[...], xc[0, :, :, cols].reshape(512, 512))
        wgr[0, :, cols] = v[0:192]
        wgr[1, :, cols] = v[192:384]
        c = xc[1, :, :, cols].reshape(512, 512)
        wgr[2, :, cols] = dot(hid_t[...], c)

    tiles(8, 512, weight_tile)
    grads_out = [
        pltpu.make_async_copy(wgr.at[k], ref, loc.at[12 + k])
        for k, ref in enumerate((gate_h, up_h, down_h))
    ]
    for copy in grads_out:
        copy.start()
    traded(0, 0)
    send_home(0)
    came_home(0)

    pulls = jnp.zeros((64, 1), F32)
    for j in range(4):
        cols = slice(1024 * j, 1024 * j + 1024)
        pulls = pulls + jnp.sum(
            pc[:, cols].astype(F32) * ret[0, :, cols].astype(F32), axis=1, keepdims=True
        )
    score = live * pulls * raw * (1.0 - raw)
    by_row = select * score
    sgt = lax.dot_general(mine16, by_row, TN, precision=HIGH, preferred_element_type=F32)
    sg = lax.dot_general(by_row, mine16, TN, precision=HIGH, preferred_element_type=F32)
    parts = jnp.concatenate([v.astype(F32) for v in thirds(sgt)], axis=0).astype(BF)
    bias = jnp.sum(sg, axis=0, keepdims=True)
    bias = jnp.concatenate([bias, jnp.zeros((1, 112), F32)], axis=1)
    bias = jnp.broadcast_to(bias, (16, 128))

    def router_tile(j, cols):
        v = dot(parts, tok[:, cols])
        core, lay = lax.rem(j, 2), lax.div(j, 2)
        t[core, lay, :, 0:512] = v[0:16] + v[16:32] + v[32:48]
        t[core, lay, :, 512:640] = bias

    tiles(8, 512, router_tile)
    sent.append(push(t.at[1 - at.c], ta, pas, par, at.partner))
    send_merged(1)
    landed(ta, par, at.partner)
    tz[...] = t[at.c] + ta[...]
    for d in range(1, 4):
        sent.append(
            push(tz.at[at.layer(d)], tzr.at[d - 1], zs.at[d - 1], zr.at[d - 1], at.at_layer(d))
        )

    w1, w2, w3 = thirds((select * gate).T)
    sg1, sg2, sg3 = thirds(sg)

    def mix_tile(j, cols):
        rows = ret[0, :, cols]
        mix[:, cols] = (dot(w1, rows) + dot(w2, rows) + dot(w3, rows)).astype(BF)
        r = router[:, cols]
        base[:, cols] = dot(sg1, r) + dot(sg2, r) + dot(sg3, r)

    tiles(8, 512, mix_tile)
    mix_out = pltpu.make_async_copy(mix, mix_h, loc.at[10])
    mix_out.start()
    traded(1, 0)
    send_home(1)
    acc = tz[at.z]
    for d in range(3):
        landed(tzr.at[d], zr.at[d], at.partner)
        acc = acc + tzr[d]
    for y in range(4):
        ext[y, :, 0:128] = acc[:, 128 * y : 128 * y + 128]
        ext[y, :, 128:256] = acc[:, 512:640]
    for d, peer in enumerate(plane):
        sent.append(push(ext.at[lax.div(peer[1], 4)], tb.at[d], sb.at[d], rbs.at[d], peer))
    came_home(1)
    select_t = select.T.astype(BF)

    def grad_tile(j, cols):
        tgr[:, cols] = (base[:, cols] + dot(select_t, ret[1, :, cols])).astype(BF)

    tiles(8, 512, grad_tile)
    grad_out = pltpu.make_async_copy(tgr, tgr_h, loc.at[11])
    grad_out.start()
    done = ext[at.y]
    for d in range(15):
        landed(tb.at[d], rbs.at[d], at.partner)
        done = done + tb[d]
    quarter = jnp.zeros((16, 32), F32)
    for x in range(4):
        quarter = jnp.where(at.x == x, done[:, 32 * x : 32 * x + 32], quarter)
    red[...] = quarter
    thr_out[...] = -done[0:1, 128:144]
    for copy in sent:
        copy.wait_send()
    for copy in grads_out:
        copy.wait()
    mix_out.wait()
    grad_out.wait()


def layer(tokens, cotangent, wg, wu, wd, router, thr, scale, picks, counts):
    vmem = pl.BlockSpec(memory_space=pltpu.VMEM)
    hbm = pl.BlockSpec(memory_space=pl.ANY)
    dma = pltpu.SemaphoreType.DMA
    v = pltpu.VMEM
    width = tokens.shape[1]
    units = wg.shape[0]
    shape = jax.ShapeDtypeStruct
    return pl.pallas_call(
        layer_kernel,
        out_shape=(
            shape((256, width), BF),
            shape((256, width), BF),
            shape((units, width), F32),
            shape((units, width), F32),
            shape((units, width), F32),
            shape((16, 32), F32),
            shape((1, 16), F32),
        ),
        in_specs=[hbm] * 5 + [vmem] * 5,
        out_specs=(hbm, hbm, hbm, hbm, hbm, vmem, vmem),
        scratch_shapes=[
            v((256, width), BF), v((256, width), BF),
            v((units, width), BF), v((units, width), BF), v((units, width), BF),
            v((64, width), BF), v((64, width), BF), v((64, width), BF),
            v((2, 16, 4, width), BF), v((2, 16, 4, width), BF),
            v((2, 32, 16, width), BF), v((2, 32, 16, width), BF),
            v((2, 4, 4, 16, width), BF), v((2, 16, 16, width), BF),
            v((2, 6, 16, width), BF), v((2, 6, 16, width), BF),
            v((2, 16, 4, width), BF), v((2, 16, 4, width), BF), v((2, 64, width), BF),
            v((512, units), F32), v((512, units), F32), v((256, units), F32),
            v((units, 512), BF), v((2 * units, 512), BF), v((3, units, width), F32),
            v((256, width), F32), v((256, width), BF), v((256, width), BF),
            v((2, 4, 16, 640), F32), v((4, 16, 640), F32), v((4, 16, 640), F32),
            v((3, 16, 640), F32), v((4, 16, 256), F32), v((15, 16, 256), F32),
            dma((2, 16)), dma((2, 16)), dma((2, 6)), dma((2, 6)), dma((2, 6)), dma((2, 6)),
            dma((2, 16)), dma((2, 16)), dma((2, 4)), dma((2, 4)),
            dma((2, 6)), dma((2, 6)), dma((2, 6)), dma((2, 6)),
            dma((2, 16)), dma((2, 16)), dma, dma, dma((3,)), dma((3,)),
            dma((15,)), dma((15,)), dma((15,)),
        ],
        compiler_params=pltpu.CompilerParams(
            collective_id=0, has_side_effects=True, vmem_limit_bytes=67043328
        ),
    )(tokens, cotangent, wg, wu, wd, router, thr, scale, picks, counts)


def on_device(tokens, cotangent, router, threshold, w_gate, w_up, w_down, hid_scale, picks, counts):
    mixture, token_grad, gate_grad, up_grad, down_grad, reduced, thresholds = layer(
        tokens, cotangent, w_gate[0].T, w_up[0].T, w_down[0], router.T,
        threshold[None, :], hid_scale, picks[0].T, counts,
    )
    return (
        mixture,
        token_grad,
        reduced.T,
        thresholds[0],
        gate_grad.T[None],
        up_grad.T[None],
        down_grad[None],
    )


def solution(mesh):
    placed = (
        P(("seq", "exp"), None),
        P(("seq", "exp"), None),
        P(),
        P(),
        P("exp", None, "seq"),
        P("exp", None, "seq"),
        P("exp", "seq", None),
        P("exp", "seq"),
        P(("seq", "exp"), None, None),
        P(("seq", "exp"), None),
    )
    return jax.shard_map(
        on_device,
        mesh=mesh,
        in_specs=placed,
        out_specs=(
            P(("seq", "exp"), None),
            P(("seq", "exp"), None),
            P(("seq", "exp"), None),
            P(),
            P("exp", None, "seq"),
            P("exp", None, "seq"),
            P("exp", "seq", None),
        ),
        check_vma=False,
    )
```

time: 151 us -> 121 us (0.80)
  Pallas kernels: 120 us -> 105 us
  matrix products: 8.15 us -> 0 us
  local copies, waits for them, and re-layouts: 20.1 us -> 13.7 us
    pallas_call x1, Pallas kernels: 120 us -> 105 us  [layer(): pl.pallas_call(layer_kernel, out_shape=(shape((256, width), BF), shape((2...]
    dot_general x3 -> x0, matrix products: 8.15 us -> none  [the longest x1 2.73 us: on_device(): lax.dot_general(expert_rows, up_delta.reshape(flat), TN, preferred_elemen...]
    slice x1 -> x0, local copies, waits for them, and re-layouts: 3.99 us -> none  [on_device(): expert_cot = rows[1].reshape(-1, features)]
    unnamed x18 -> x19, local copies, waits for them, and re-layouts: 13 us -> 13.7 us
where the time goes in v3:
time: 121 us; the launch traced here: 120 us
  Pallas kernels  105 us (87%)
  local copies, waits for them, and re-layouts  13.7 us (11%)
    pallas_call x1, Pallas kernels, layer(): pl.pallas_call(layer_kernel, out_shape=(shape((256, width), BF), shape((2...  105 us
    unnamed x19, local copies, waits for them, and re-layouts  13.7 us

profile of v3, /device:TPU:0, one launch (start us, length us, event | category | flops | bytes accessed | tf_op | source)
XLA Modules:
  0.0 119.6 jit_solution(3494376651676154889)
XLA Ops:
  0.6 105.3 %shard_map.153 = (bf16[256,4096]{1,0:T(8,128)(2,1)}, bf16[256,4096]{1,0:T(8,128)(2,1)}, f32[192,4096]{1,0:T(8,128)}, f32[192,4096]{1,0:T(8,128)}, f32[192,4096]{...) custom-call(bf16[256,4096]{1,0:T(8,128)(2,1)} %tok_h.1, bf16[256,4096]{1,0:T(8,128)(2,1)} %cot_h.1, ...), custom_call_target="tpu_custom_call" | custom-call | tf_op jit(solution)/shard_map/pallas_call | solution.py:554
  105.9 0.0 copy-start.3
  105.9 3.3 %copy.24 = bf16[256,4096]{1,0:T(8,128)(2,1)} copy(bf16[256,4096]{1,0:T(8,128)(2,1)} %get-tuple-element.28) | data formatting | bytes 4194304
  109.2 0.0 copy-done.3
  109.2 0.0 copy-start.4
  109.2 0.0 copy-start.5
  109.2 0.0 copy-start.2
  109.2 1.3 %copy.25 = bf16[256,4096]{1,0:T(8,128)(2,1)} copy(bf16[256,4096]{1,0:T(8,128)(2,1)S(1)} %copy-done.3) | data formatting | bytes 4194304
  110.6 0.0 copy-done.4
  110.6 0.6 copy.26
  111.2 0.0 copy-done.5
  111.2 0.5 copy.27
  111.7 0.2 copy-done.2
  111.9 0.0 copy-start.1
  111.9 1.7 %copy.28 = f32[1,4096,192]{1,2,0:T(8,128)} copy(f32[1,4096,192]{1,2,0:T(8,128)S(1)} %bitcast.23) | data formatting | bytes 6291456
  113.6 1.4 %copy-done.1 = f32[192,4096]{1,0:T(8,128)S(1)} copy-done((f32[192,4096]{1,0:T(8,128)S(1)}, f32[192,4096]{1,0:T(8,128)}, u32[]{:S(2)}) %copy-start.1) | copy-done | bytes 3145752
  114.9 0.0 copy-start
  114.9 1.7 %copy.29 = f32[1,4096,192]{1,2,0:T(8,128)} copy(f32[1,4096,192]{1,2,0:T(8,128)S(1)} %bitcast.22) | data formatting | bytes 6291456
  116.6 1.4 %copy-done = f32[192,4096]{1,0:T(8,128)S(1)} copy-done((f32[192,4096]{1,0:T(8,128)S(1)}, f32[192,4096]{1,0:T(8,128)}, u32[]{:S(2)}) %copy-start) | copy-done | bytes 3145752
  117.9 1.7 %copy.30 = f32[1,192,4096]{2,1,0:T(8,128)} copy(f32[1,192,4096]{2,1,0:T(8,128)S(1)} %bitcast.21) | data formatting | bytes 6291456
Async XLA Ops:
  105.9 3.3 %copy-start.3 = (bf16[256,4096]{1,0:T(8,128)(2,1)S(1)}, bf16[256,4096]{1,0:T(8,128)(2,1)}, u32[]{:S(2)}) copy-start(bf16[256,4096]{1,0:T(8,128)(2,1)} %get-tuple-element.29) | copy-start | bytes 6291460
  109.2 1.3 %copy-start.4 = (f32[16,32]{1,0:T(8,128)S(1)}, f32[16,32]{1,0:T(8,128)}, u32[]{:S(2)}) copy-start(f32[16,32]{1,0:T(8,128)} %get-tuple-element.16) | copy-start | bytes 6148
  109.2 1.9 %copy-start.5 = (f32[1,16]{1,0:T(1,128)S(1)}, f32[1,16]{1,0:T(1,128)}, u32[]{:S(2)}) copy-start(f32[1,16]{1,0:T(1,128)} %get-tuple-element.17) | copy-start | bytes 196
  109.2 2.7 %copy-start.2 = (f32[192,4096]{1,0:T(8,128)S(1)}, f32[192,4096]{1,0:T(8,128)}, u32[]{:S(2)}) copy-start(f32[192,4096]{1,0:T(8,128)} %get-tuple-element.18) | copy-start | bytes 9437188
  111.9 3.0 %copy-start.1 = (f32[192,4096]{1,0:T(8,128)S(1)}, f32[192,4096]{1,0:T(8,128)}, u32[]{:S(2)}) copy-start(f32[192,4096]{1,0:T(8,128)} %get-tuple-element.19) | copy-start | bytes 9437188
  114.9 3.0 %copy-start = (f32[192,4096]{1,0:T(8,128)S(1)}, f32[192,4096]{1,0:T(8,128)}, u32[]{:S(2)}) copy-start(f32[192,4096]{1,0:T(8,128)} %get-tuple-element.20) | copy-start | bytes 9437188

commit v4 on v3

--- a/solution.py
+++ b/solution.py
@@ -9,7 +9,7 @@
 BF = jnp.bfloat16
 F32 = jnp.float32
 HIGH = lax.Precision.HIGHEST
-UP = (0, 2)
+UP = (2, 0)
 DOWN = (1, 3)
 
 
@@ -107,11 +107,15 @@
     lax.fori_loop(0, count, step, 0)
 
 
+def joined(pieces, axis):
+    return jnp.concatenate([v.astype(F32) for v in pieces], axis=axis).astype(BF)
+
+
 def layer_kernel(
     tok_h, cot_h, wg_h, wu_h, wd_h, router, thr, scale, picks, counts,
-    mix_h, tgr_h, gate_h, up_h, down_h, red, thr_out,
-    tok, cot, wg, wu, wd, xr, cr, pc, msg, buf, xc, pp, pb, tot, xp, xm, om, rb, ret,
-    pre_g, pre_u, hg, hid_t, del_t, wgr, base, mix, tgr, t, ta, tz, tzr, ext, tb,
+    mix, tgr, gate_w, up_w, down_w, red, thr_out,
+    tok, cot, wg, wu, wd, xr, cr, pc, msg, buf, xc, pp, pb, xp, xm, om, rb, ret,
+    pre_g, pre_u, hg, hid_t, del_t, base, t, ta, tz, tzr, ext, tb,
     s1, r1, sp, rp, sm, rm, sq, rq, es, er, tps, tpr, tms, tmr, s3, r3,
     pas, par, zs, zr, sb, rbs, loc,
 ):
@@ -121,11 +125,13 @@
     greet(plane + column)
     loads = [
         pltpu.make_async_copy(a, b, loc.at[k])
-        for k, (a, b) in enumerate(
-            [(tok_h, tok), (cot_h, cot), (wg_h, wg), (wu_h, wu), (wd_h, wd)]
-        )
+        for k, (a, b) in enumerate([(cot_h, cot), (wg_h, wg), (wu_h, wu), (wd_h, wd)])
     ]
-    loads[0].start()
+    pieces = []
+    for k in range(4):
+        cols = slice(1024 * k, 1024 * k + 1024)
+        pieces.append(pltpu.make_async_copy(tok_h.at[:, cols], tok.at[:, cols], loc.at[9 + k]))
+        pieces[k].start()
 
     row = lax.broadcasted_iota(jnp.int32, (64, 16), 0)
     lane = lax.broadcasted_iota(jnp.int32, (64, 16), 1)
@@ -142,13 +148,12 @@
         pick == lax.broadcasted_iota(jnp.int32, (64, 256), 1).astype(F32)
     ).astype(F32)
     select_bf = select.astype(BF)
-    loads[0].wait()
-    loads[1].start()
-
-    def take_rows(j, cols):
+    loads[0].start()
+
+    for k in range(4):
+        cols = slice(1024 * k, 1024 * k + 1024)
+        pieces[k].wait()
         xr[:, cols] = dot(select_bf, tok[:, cols]).astype(BF)
-
-    tiles(8, 512, take_rows)
     for e in range(16):
         msg[0, e] = xr[4 * e : 4 * e + 4, :]
     greeted(22)
@@ -177,8 +182,8 @@
     chosen_gates = jnp.dot(select, gates, precision=HIGH, preferred_element_type=F32)
     raw = jnp.sum(chosen_gates * mine16, axis=1, keepdims=True)
     gate = raw * live
-    loads[1].wait()
-    for load in loads[2:]:
+    loads[0].wait()
+    for load in loads[1:]:
         load.start()
 
     def take_cots(j, cols):
@@ -315,17 +320,16 @@
         landed(pb.at[kind, up], er.at[kind, up], at.partner)
 
     def combine(kind, up, i, extra):
-        q = up * 4 + i
         parts = [pp.at[kind, at.slot(up, 0, i)], pb.at[kind, up, at.group(i)]] + extra
 
         def add(j, cols):
             acc = parts[0][:, cols].astype(F32)
             for part in parts[1:]:
                 acc = acc + part[:, cols].astype(F32)
-            tot[kind, q, :, cols] = acc.astype(BF)
+            parts[1][:, cols] = acc.astype(BF)
 
         tiles(4, 1024, add)
-        return tot.at[kind, q]
+        return parts[1]
 
     def up_send(kind, src, k):
         sent.append(push(src, xp.at[kind, k], tps.at[kind, k], tpr.at[kind, k], at.above))
@@ -357,11 +361,12 @@
             down_send(kind, combine(kind, 3, DOWN[k], [from_above(kind, 2 + k)]), 4 + k)
 
     def send_home(kind):
-        for i in (1, 0, 3, 2):
-            k = i // 2
+        for i in (DOWN[0], UP[0], DOWN[1], UP[1]):
             if i in UP:
+                k = UP.index(i)
                 extra = [from_above(kind, k), from_below(kind, 4 + k)]
             else:
+                k = DOWN.index(i)
                 extra = [from_below(kind, k), from_above(kind, 4 + k)]
             sums = combine(kind, 0, i, extra)
             for x in range(4):
@@ -396,50 +401,50 @@
     gather(1, 2)
     gather(1, 3)
     from_partner(0, 0)
-    for load in loads[2:]:
+    for load in loads[1:]:
         load.wait()
     forward(0)
     trade(0, 0)
     from_beside(0, 2)
     from_beside(0, 3)
-    from_across(0, 0)
-    from_across(0, 1)
     from_partner(0, 3)
     from_partner(0, 1)
     forward(1, 3)
     trade(0, 1)
     trade(0, 3)
+    from_across(0, 0)
+    from_across(0, 1)
     from_beside(1, 0)
     from_beside(1, 1)
-    from_across(0, 2)
-    from_across(0, 3)
     traded(0, 1)
     traded(0, 3)
     send_plain(0)
+    from_partner(1, 0)
+    backward(0)
+    trade(1, 0)
+    from_beside(1, 2)
+    from_beside(1, 3)
+    from_across(0, 2)
+    from_across(0, 3)
     from_partner(0, 2)
     forward(2)
     trade(0, 2)
-    from_beside(1, 2)
-    from_beside(1, 3)
-    from_partner(1, 0)
+    from_across(1, 0)
+    from_across(1, 1)
     traded(0, 2)
     send_across(0)
-    from_across(1, 0)
-    from_across(1, 1)
-    backward(0)
-    trade(1, 0)
-    from_across(1, 2)
-    from_across(1, 3)
     from_partner(1, 3)
     from_partner(1, 1)
     backward(1, 3)
     trade(1, 1)
     trade(1, 3)
+    from_across(1, 2)
+    from_across(1, 3)
     send_merged(0)
-    from_partner(1, 2)
     traded(1, 1)
     traded(1, 3)
     send_plain(1)
+    from_partner(1, 2)
     backward(2)
     trade(1, 2)
     traded(1, 2)
@@ -447,20 +452,15 @@
 
     def weight_tile(j, cols):
         v = dot(del_t[...], xc[0, :, :, cols].reshape(512, 512))
-        wgr[0, :, cols] = v[0:192]
-        wgr[1, :, cols] = v[192:384]
+        gate_w[:, cols] = v[0:192]
+        up_w[:, cols] = v[192:384]
         c = xc[1, :, :, cols].reshape(512, 512)
-        wgr[2, :, cols] = dot(hid_t[...], c)
+        down_w[:, cols] = dot(hid_t[...], c)
 
     tiles(8, 512, weight_tile)
-    grads_out = [
-        pltpu.make_async_copy(wgr.at[k], ref, loc.at[12 + k])
-        for k, ref in enumerate((gate_h, up_h, down_h))
-    ]
-    for copy in grads_out:
-        copy.start()
     traded(0, 0)
     send_home(0)
+    send_merged(1)
     came_home(0)
 
     pulls = jnp.zeros((64, 1), F32)
@@ -473,7 +473,7 @@
     by_row = select * score
     sgt = lax.dot_general(mine16, by_row, TN, precision=HIGH, preferred_element_type=F32)
     sg = lax.dot_general(by_row, mine16, TN, precision=HIGH, preferred_element_type=F32)
-    parts = jnp.concatenate([v.astype(F32) for v in thirds(sgt)], axis=0).astype(BF)
+    parts = joined(thirds(sgt), 0)
     bias = jnp.sum(sg, axis=0, keepdims=True)
     bias = jnp.concatenate([bias, jnp.zeros((1, 112), F32)], axis=1)
     bias = jnp.broadcast_to(bias, (16, 128))
@@ -486,28 +486,22 @@
 
     tiles(8, 512, router_tile)
     sent.append(push(t.at[1 - at.c], ta, pas, par, at.partner))
-    send_merged(1)
+    traded(1, 0)
+    send_home(1)
     landed(ta, par, at.partner)
     tz[...] = t[at.c] + ta[...]
     for d in range(1, 4):
         sent.append(
             push(tz.at[at.layer(d)], tzr.at[d - 1], zs.at[d - 1], zr.at[d - 1], at.at_layer(d))
         )
-
-    w1, w2, w3 = thirds((select * gate).T)
-    sg1, sg2, sg3 = thirds(sg)
+    mix_w = joined(thirds((select * gate).T), 1)
+    sg_w = joined(thirds(sg), 1)
 
     def mix_tile(j, cols):
         rows = ret[0, :, cols]
-        mix[:, cols] = (dot(w1, rows) + dot(w2, rows) + dot(w3, rows)).astype(BF)
-        r = router[:, cols]
-        base[:, cols] = dot(sg1, r) + dot(sg2, r) + dot(sg3, r)
+        mix[:, cols] = dot(mix_w, jnp.concatenate([rows] * 3, axis=0)).astype(BF)
 
     tiles(8, 512, mix_tile)
-    mix_out = pltpu.make_async_copy(mix, mix_h, loc.at[10])
-    mix_out.start()
-    traded(1, 0)
-    send_home(1)
     acc = tz[at.z]
     for d in range(3):
         landed(tzr.at[d], zr.at[d], at.partner)
@@ -517,6 +511,14 @@
         ext[y, :, 128:256] = acc[:, 512:640]
     for d, peer in enumerate(plane):
         sent.append(push(ext.at[lax.div(peer[1], 4)], tb.at[d], sb.at[d], rbs.at[d], peer))
+
+    def base_tile(j, cols):
+        r = router[:, cols]
+        base[:, cols] = dot(sg_w, jnp.concatenate([r] * 3, axis=0))
+
+    tiles(8, 512, base_tile)
+    for copy in sent:
+        copy.wait_send()
     came_home(1)
     select_t = select.T.astype(BF)
 
@@ -524,8 +526,6 @@
         tgr[:, cols] = (base[:, cols] + dot(select_t, ret[1, :, cols])).astype(BF)
 
     tiles(8, 512, grad_tile)
-    grad_out = pltpu.make_async_copy(tgr, tgr_h, loc.at[11])
-    grad_out.start()
     done = ext[at.y]
     for d in range(15):
         landed(tb.at[d], rbs.at[d], at.partner)
@@ -535,12 +535,6 @@
         quarter = jnp.where(at.x == x, done[:, 32 * x : 32 * x + 32], quarter)
     red[...] = quarter
     thr_out[...] = -done[0:1, 128:144]
-    for copy in sent:
-        copy.wait_send()
-    for copy in grads_out:
-        copy.wait()
-    mix_out.wait()
-    grad_out.wait()
 
 
 def layer(tokens, cotangent, wg, wu, wd, router, thr, scale, picks, counts):
@@ -550,42 +544,41 @@
     v = pltpu.VMEM
     width = tokens.shape[1]
     units = wg.shape[0]
-    shape = jax.ShapeDtypeStruct
     return pl.pallas_call(
         layer_kernel,
         out_shape=(
-            shape((256, width), BF),
-            shape((256, width), BF),
-            shape((units, width), F32),
-            shape((units, width), F32),
-            shape((units, width), F32),
-            shape((16, 32), F32),
-            shape((1, 16), F32),
+            v((256, width), BF),
+            v((256, width), BF),
+            v((units, width), F32),
+            v((units, width), F32),
+            v((units, width), F32),
+            v((16, 32), F32),
+            v((1, 16), F32),
         ),
         in_specs=[hbm] * 5 + [vmem] * 5,
-        out_specs=(hbm, hbm, hbm, hbm, hbm, vmem, vmem),
+        out_specs=(vmem,) * 7,
         scratch_shapes=[
             v((256, width), BF), v((256, width), BF),
             v((units, width), BF), v((units, width), BF), v((units, width), BF),
             v((64, width), BF), v((64, width), BF), v((64, width), BF),
             v((2, 16, 4, width), BF), v((2, 16, 4, width), BF),
             v((2, 32, 16, width), BF), v((2, 32, 16, width), BF),
-            v((2, 4, 4, 16, width), BF), v((2, 16, 16, width), BF),
+            v((2, 4, 4, 16, width), BF),
             v((2, 6, 16, width), BF), v((2, 6, 16, width), BF),
             v((2, 16, 4, width), BF), v((2, 16, 4, width), BF), v((2, 64, width), BF),
             v((512, units), F32), v((512, units), F32), v((256, units), F32),
-            v((units, 512), BF), v((2 * units, 512), BF), v((3, units, width), F32),
-            v((256, width), F32), v((256, width), BF), v((256, width), BF),
+            v((units, 512), BF), v((2 * units, 512), BF),
+            v((256, width), F32),
             v((2, 4, 16, 640), F32), v((4, 16, 640), F32), v((4, 16, 640), F32),
             v((3, 16, 640), F32), v((4, 16, 256), F32), v((15, 16, 256), F32),
             dma((2, 16)), dma((2, 16)), dma((2, 6)), dma((2, 6)), dma((2, 6)), dma((2, 6)),
             dma((2, 16)), dma((2, 16)), dma((2, 4)), dma((2, 4)),
             dma((2, 6)), dma((2, 6)), dma((2, 6)), dma((2, 6)),
             dma((2, 16)), dma((2, 16)), dma, dma, dma((3,)), dma((3,)),
-            dma((15,)), dma((15,)), dma((15,)),
+            dma((15,)), dma((15,)), dma((13,)),
         ],
         compiler_params=pltpu.CompilerParams(
-            collective_id=0, has_side_effects=True, vmem_limit_bytes=67043328
+            collective_id=0, has_side_effects=True, vmem_limit_bytes=49 << 20
         ),
     )(tokens, cotangent, wg, wu, wd, router, thr, scale, picks, counts)
 

time: 121 us -> 106 us (0.88)
  Pallas kernels: 105 us -> 96.3 us
  local copies, waits for them, and re-layouts: 13.7 us -> 8.74 us
    pallas_call x1, Pallas kernels: 105 us -> 96.3 us  [layer(): pl.pallas_call(layer_kernel, out_shape=(v((256, width), BF), v((256, widt...]
    unnamed x19 -> x7, local copies, waits for them, and re-layouts: 13.7 us -> 8.74 us
where the time goes in v4:
time: 106 us
  Pallas kernels  96.3 us (91%)
  local copies, waits for them, and re-layouts  8.74 us (8%)
    pallas_call x1, Pallas kernels, layer(): pl.pallas_call(layer_kernel, out_shape=(v((256, width), BF), v((256, widt...  96.3 us
    unnamed x7, local copies, waits for them, and re-layouts  8.74 us

profile of v4, /device:TPU:0, one launch (start us, length us, event | category | flops | bytes accessed | tf_op | source)
XLA Modules:
  0.0 105.7 jit_solution(5144246079247369015)
XLA Ops:
  0.6 96.3 %shard_map.153 = (bf16[256,4096]{1,0:T(8,128)(2,1)S(1)}, bf16[256,4096]{1,0:T(8,128)(2,1)S(1)}, f32[192,4096]{1,0:T(8,128)S(1)}, f32[192,4096]{1,0:T(8,128)S(1)}...) custom-call(bf16[256,4096]{1,0:T(8,128)(2,1)} %tok_h.1, bf16[256,4096]{1,0:T(8,128)(2,1)} %cot_h.1, ...), custom_call_target="tpu_custom_call" | custom-call | tf_op jit(solution)/shard_map/pallas_call | solution.py:547
  96.9 1.3 %copy.24 = bf16[256,4096]{1,0:T(8,128)(2,1)} copy(bf16[256,4096]{1,0:T(8,128)(2,1)S(1)} %get-tuple-element.21) | data formatting | bytes 4194304
  98.2 0.5 copy.27
  98.7 0.6 copy.26
  99.3 1.3 %copy.25 = bf16[256,4096]{1,0:T(8,128)(2,1)} copy(bf16[256,4096]{1,0:T(8,128)(2,1)S(1)} %get-tuple-element.22) | data formatting | bytes 4194304
  100.7 1.7 %copy.28 = f32[1,4096,192]{1,2,0:T(8,128)} copy(f32[1,4096,192]{1,2,0:T(8,128)S(1)} %bitcast.23) | data formatting | bytes 6291456
  102.3 1.7 %copy.29 = f32[1,4096,192]{1,2,0:T(8,128)} copy(f32[1,4096,192]{1,2,0:T(8,128)S(1)} %bitcast.22) | data formatting | bytes 6291456
  104.0 1.7 %copy.30 = f32[1,192,4096]{2,1,0:T(8,128)} copy(f32[1,192,4096]{2,1,0:T(8,128)S(1)} %bitcast.21) | data formatting | bytes 6291456

commit v5 on v4

--- a/solution.py
+++ b/solution.py
@@ -440,13 +440,13 @@
     trade(1, 3)
     from_across(1, 2)
     from_across(1, 3)
-    send_merged(0)
     traded(1, 1)
     traded(1, 3)
     send_plain(1)
     from_partner(1, 2)
     backward(2)
     trade(1, 2)
+    send_merged(0)
     traded(1, 2)
     send_across(1)
 
@@ -486,32 +486,31 @@
 
     tiles(8, 512, router_tile)
     sent.append(push(t.at[1 - at.c], ta, pas, par, at.partner))
-    traded(1, 0)
-    send_home(1)
     landed(ta, par, at.partner)
     tz[...] = t[at.c] + ta[...]
     for d in range(1, 4):
         sent.append(
             push(tz.at[at.layer(d)], tzr.at[d - 1], zs.at[d - 1], zr.at[d - 1], at.at_layer(d))
         )
-    mix_w = joined(thirds((select * gate).T), 1)
-    sg_w = joined(thirds(sg), 1)
-
-    def mix_tile(j, cols):
-        rows = ret[0, :, cols]
-        mix[:, cols] = dot(mix_w, jnp.concatenate([rows] * 3, axis=0)).astype(BF)
-
-    tiles(8, 512, mix_tile)
+    traded(1, 0)
+    send_home(1)
     acc = tz[at.z]
     for d in range(3):
         landed(tzr.at[d], zr.at[d], at.partner)
         acc = acc + tzr[d]
     for y in range(4):
-        ext[y, :, 0:128] = acc[:, 128 * y : 128 * y + 128]
-        ext[y, :, 128:256] = acc[:, 512:640]
+        ext[y, 0:16, :] = acc[:, 128 * y : 128 * y + 128]
+        ext[y, 16:24, :] = acc[0:8, 512:640]
     for d, peer in enumerate(plane):
         sent.append(push(ext.at[lax.div(peer[1], 4)], tb.at[d], sb.at[d], rbs.at[d], peer))
-
+    mix_w = joined(thirds((select * gate).T), 1)
+    sg_w = joined(thirds(sg), 1)
+
+    def mix_tile(j, cols):
+        rows = ret[0, :, cols]
+        mix[:, cols] = dot(mix_w, jnp.concatenate([rows] * 3, axis=0)).astype(BF)
+
+    tiles(8, 512, mix_tile)
     def base_tile(j, cols):
         r = router[:, cols]
         base[:, cols] = dot(sg_w, jnp.concatenate([r] * 3, axis=0))
@@ -532,9 +531,9 @@
         done = done + tb[d]
     quarter = jnp.zeros((16, 32), F32)
     for x in range(4):
-        quarter = jnp.where(at.x == x, done[:, 32 * x : 32 * x + 32], quarter)
+        quarter = jnp.where(at.x == x, done[0:16, 32 * x : 32 * x + 32], quarter)
     red[...] = quarter
-    thr_out[...] = -done[0:1, 128:144]
+    thr_out[...] = -done[16:17, 0:16]
 
 
 def layer(tokens, cotangent, wg, wu, wd, router, thr, scale, picks, counts):
@@ -570,7 +569,7 @@
             v((units, 512), BF), v((2 * units, 512), BF),
             v((256, width), F32),
             v((2, 4, 16, 640), F32), v((4, 16, 640), F32), v((4, 16, 640), F32),
-            v((3, 16, 640), F32), v((4, 16, 256), F32), v((15, 16, 256), F32),
+            v((3, 16, 640), F32), v((4, 24, 128), F32), v((15, 24, 128), F32),
             dma((2, 16)), dma((2, 16)), dma((2, 6)), dma((2, 6)), dma((2, 6)), dma((2, 6)),
             dma((2, 16)), dma((2, 16)), dma((2, 4)), dma((2, 4)),
             dma((2, 6)), dma((2, 6)), dma((2, 6)), dma((2, 6)),
@@ -583,11 +582,36 @@
     )(tokens, cotangent, wg, wu, wd, router, thr, scale, picks, counts)
 
 
+def store_kernel(*refs):
+    half = len(refs) // 2
+    sems = refs[-1]
+    copies = [
+        pltpu.make_async_copy(refs[k], refs[half + k], sems.at[k]) for k in range(half)
+    ]
+    for copy in copies:
+        copy.start()
+    for copy in copies:
+        copy.wait()
+
+
+def store(values):
+    held = [pltpu.with_memory_space_constraint(a, pltpu.VMEM) for a in values]
+    return pl.pallas_call(
+        store_kernel,
+        out_shape=tuple(jax.ShapeDtypeStruct(a.shape, a.dtype) for a in values),
+        in_specs=[pl.BlockSpec(memory_space=pltpu.VMEM)] * len(values),
+        out_specs=tuple(pl.BlockSpec(memory_space=pl.ANY) for _ in values),
+        scratch_shapes=[pltpu.SemaphoreType.DMA((len(values),))],
+        compiler_params=pltpu.CompilerParams(vmem_limit_bytes=8 << 20),
+    )(*held)
+
+
 def on_device(tokens, cotangent, router, threshold, w_gate, w_up, w_down, hid_scale, picks, counts):
-    mixture, token_grad, gate_grad, up_grad, down_grad, reduced, thresholds = layer(
+    results = layer(
         tokens, cotangent, w_gate[0].T, w_up[0].T, w_down[0], router.T,
         threshold[None, :], hid_scale, picks[0].T, counts,
     )
+    mixture, token_grad, gate_grad, up_grad, down_grad, reduced, thresholds = store(results)
     return (
         mixture,
         token_grad,

time: 106 us -> 101 us (0.953); the launches traced: 106 us -> 99.4 us
  local copies, waits for them, and re-layouts: 8.74 us -> 0 us
  Pallas kernels: 96.3 us -> 98.8 us
    unnamed x7 -> x0, local copies, waits for them, and re-layouts: 8.74 us -> none
    pallas_call x0 -> x1, Pallas kernels: none -> 5.01 us  [store(): pl.pallas_call(store_kernel, out_shape=tuple((jax.ShapeDtypeStruct(a.shap...]
    pallas_call x1, Pallas kernels: 96.3 us -> 93.8 us  [layer(): pl.pallas_call(layer_kernel, out_shape=(v((256, width), BF), v((256, widt...]
where the time goes in v5:
time: 101 us; the launch traced here: 99.4 us
  Pallas kernels  98.8 us (98%)
    pallas_call x1, Pallas kernels, layer(): pl.pallas_call(layer_kernel, out_shape=(v((256, width), BF), v((256, widt...  93.8 us
    pallas_call x1, Pallas kernels, store(): pl.pallas_call(store_kernel, out_shape=tuple((jax.ShapeDtypeStruct(a.shap...  5.01 us

profile of v5, /device:TPU:0, one launch (start us, length us, event | category | flops | bytes accessed | tf_op | source)
XLA Modules:
  0.0 99.4 jit_solution(3766206338362694353)
XLA Ops:
  0.6 93.8 %shard_map.153 = (bf16[256,4096]{1,0:T(8,128)(2,1)S(1)}, bf16[256,4096]{1,0:T(8,128)(2,1)S(1)}, f32[192,4096]{1,0:T(8,128)S(1)}, f32[192,4096]{1,0:T(8,128)S(1)}...) custom-call(bf16[256,4096]{1,0:T(8,128)(2,1)} %tok_h.1, bf16[256,4096]{1,0:T(8,128)(2,1)} %cot_h.1, ...), custom_call_target="tpu_custom_call" | custom-call | tf_op jit(solution)/shard_map/pallas_call | solution.py:546
  94.4 5.0 %shard_map.154 = (bf16[256,4096]{1,0:T(8,128)(2,1)}, bf16[256,4096]{1,0:T(8,128)(2,1)}, f32[192,4096]{1,0:T(8,128)}, f32[192,4096]{1,0:T(8,128)}, f32[192,4096]{...) custom-call(bf16[256,4096]{1,0:T(8,128)(2,1)S(1)} %get-tuple-element.21.refs_0_, ...), custom_call_target="tpu_custom_call" | custom-call | tf_op jit(solution)/shard_map/pallas_call | solution.py:599

commit v6 on v5

--- a/solution.py
+++ b/solution.py
@@ -105,6 +105,17 @@
         return carry
 
     lax.fori_loop(0, count, step, 0)
+
+
+def left(ref, send_sem, device):
+    pltpu.make_async_remote_copy(
+        src_ref=ref,
+        dst_ref=ref,
+        send_sem=send_sem,
+        recv_sem=send_sem,
+        device_id=device,
+        device_id_type=MESH,
+    ).wait_send()
 
 
 def joined(pieces, axis):
@@ -166,10 +177,9 @@
         for i, j in HOPS:
             if i or j:
                 e = at.in_plane(4 - i, j)
-                k = i * 4 + j
                 sent.append(
                     push(
-                        msg.at[kind, e], buf.at[kind, at.e], s1.at[kind, k], r1.at[kind, k],
+                        msg.at[kind, e], buf.at[kind, at.e], s1.at[kind], r1.at[kind, i],
                         (at.s, e),
                     )
                 )
@@ -198,22 +208,21 @@
 
     def hand_over(kind, slot, q):
         ref = xc.at[kind, slot]
-        sent.append(push(ref, ref, sq.at[kind, q], rq.at[kind, q], at.partner))
+        push(ref, ref, sq.at[kind], rq.at[kind, q // 4], at.partner)
 
     def climb(kind, slot, k):
         ref = xc.at[kind, slot]
-        sent.append(push(ref, ref, sp.at[kind, k], rp.at[kind, k], at.above))
+        push(ref, ref, sp.at[kind], rp.at[kind, k], at.above)
 
     def sink(kind, slot, k):
         ref = xc.at[kind, slot]
-        sent.append(push(ref, ref, sm.at[kind, k], rm.at[kind, k], at.below))
+        push(ref, ref, sm.at[kind], rm.at[kind, k], at.below)
 
     def gather(kind, i):
         group = at.group(i)
         slot = at.slot(0, 0, i)
-        for j in range(4):
-            if i or j:
-                landed(buf.at[kind, at.in_plane(i, 4 - j)], r1.at[kind, i * 4 + j], at.partner)
+        came = pl.ds(group * 4, 4 if i else 3)
+        landed(buf.at[kind, came], r1.at[kind, i], at.partner)
         for x in range(4):
             xc[kind, slot, 4 * x : 4 * x + 4, :] = buf[kind, group * 4 + x]
         climb(kind, slot, i)
@@ -241,9 +250,8 @@
         hand_over(kind, slot, 12 + i)
 
     def from_partner(kind, up):
-        first = (0, 8, 12, 4)[up]
-        for i in range(4):
-            landed(xc.at[kind, at.slot(up, 1, i)], rq.at[kind, first + i], at.partner)
+        slots = pl.ds(at.slot(up, 1, 0) - at.y, 4)
+        landed(xc.at[kind, slots], rq.at[kind, (0, 2, 3, 1)[up]], at.partner)
 
     def stacked(kind, lays, cols, width):
         parts = [xc[kind, pl.ds(lay * 8, 8), :, cols].reshape(128, width) for lay in lays]
@@ -313,7 +321,7 @@
     def trade(kind, up):
         slots = pl.ds(at.slot(up, 1, 0) - at.y, 4)
         sent.append(
-            push(pp.at[kind, slots], pb.at[kind, up], es.at[kind, up], er.at[kind, up], at.partner)
+            push(pp.at[kind, slots], pb.at[kind, up], es.at[kind], er.at[kind, up], at.partner)
         )
 
     def traded(kind, up):
@@ -332,10 +340,10 @@
         return parts[1]
 
     def up_send(kind, src, k):
-        sent.append(push(src, xp.at[kind, k], tps.at[kind, k], tpr.at[kind, k], at.above))
+        push(src, xp.at[kind, k], tps.at[kind], tpr.at[kind, k], at.above)
 
     def down_send(kind, src, k):
-        sent.append(push(src, xm.at[kind, k], tms.at[kind, k], tmr.at[kind, k], at.below))
+        push(src, xm.at[kind, k], tms.at[kind], tmr.at[kind, k], at.below)
 
     def from_below(kind, k):
         landed(xp.at[kind, k], tpr.at[kind, k], at.above)
@@ -374,21 +382,16 @@
             for j in (1, 3, 2, 0):
                 e = at.in_plane(i, j)
                 src = om.at[kind, i * 4 + lax.rem(at.x + j, 4)]
-                k = i * 4 + j
-                if k:
+                if i or j:
                     sent.append(
-                        push(src, rb.at[kind, at.e], s3.at[kind, k], r3.at[kind, k], (at.s, e))
+                        push(src, rb.at[kind, at.e], s3.at[kind], r3.at[kind], (at.s, e))
                     )
                 else:
                     pltpu.make_async_copy(src, rb.at[kind, at.e], loc.at[7 + kind]).start()
 
     def came_home(kind):
-        for i, j in HOPS:
-            e = at.in_plane(4 - i, 4 - j)
-            if i or j:
-                landed(rb.at[kind, e], r3.at[kind, i * 4 + j], at.partner)
-            else:
-                pltpu.make_async_copy(om.at[kind, at.x], rb.at[kind, e], loc.at[7 + kind]).wait()
+        pltpu.make_async_copy(om.at[kind, at.x], rb.at[kind, at.e], loc.at[7 + kind]).wait()
+        landed(rb.at[kind, 0:15], r3.at[kind], at.partner)
         for e in range(16):
             ret[kind, 4 * e : 4 * e + 4, :] = rb[kind, e]
 
@@ -485,24 +488,24 @@
         t[core, lay, :, 512:640] = bias
 
     tiles(8, 512, router_tile)
-    sent.append(push(t.at[1 - at.c], ta, pas, par, at.partner))
+    push(t.at[1 - at.c], ta, pas, par, at.partner)
     landed(ta, par, at.partner)
     tz[...] = t[at.c] + ta[...]
     for d in range(1, 4):
         sent.append(
-            push(tz.at[at.layer(d)], tzr.at[d - 1], zs.at[d - 1], zr.at[d - 1], at.at_layer(d))
+            push(tz.at[at.layer(d)], tzr.at[d - 1], zs, zr, at.at_layer(d))
         )
     traded(1, 0)
     send_home(1)
     acc = tz[at.z]
+    landed(tzr, zr, at.partner)
     for d in range(3):
-        landed(tzr.at[d], zr.at[d], at.partner)
         acc = acc + tzr[d]
     for y in range(4):
         ext[y, 0:16, :] = acc[:, 128 * y : 128 * y + 128]
         ext[y, 16:24, :] = acc[0:8, 512:640]
     for d, peer in enumerate(plane):
-        sent.append(push(ext.at[lax.div(peer[1], 4)], tb.at[d], sb.at[d], rbs.at[d], peer))
+        push(ext.at[lax.div(peer[1], 4)], tb.at[d], sb, rbs, peer)
     mix_w = joined(thirds((select * gate).T), 1)
     sg_w = joined(thirds(sg), 1)
 
@@ -516,8 +519,18 @@
         base[:, cols] = dot(sg_w, jnp.concatenate([r] * 3, axis=0))
 
     tiles(8, 512, base_tile)
-    for copy in sent:
-        copy.wait_send()
+    for kind in range(2):
+        left(msg.at[kind, 0:15], s1.at[kind], at.partner)
+        left(xc.at[kind, 0:6], sp.at[kind], at.partner)
+        left(xc.at[kind, 0:6], sm.at[kind], at.partner)
+        left(xc.at[kind, 0:16], sq.at[kind], at.partner)
+        left(pb.at[kind], es.at[kind], at.partner)
+        left(xp.at[kind], tps.at[kind], at.partner)
+        left(xm.at[kind], tms.at[kind], at.partner)
+        left(om.at[kind, 0:15], s3.at[kind], at.partner)
+    left(ta, pas, at.partner)
+    left(tzr, zs, at.partner)
+    left(tb, sb, at.partner)
     came_home(1)
     select_t = select.T.astype(BF)
 
@@ -526,8 +539,8 @@
 
     tiles(8, 512, grad_tile)
     done = ext[at.y]
+    landed(tb, rbs, at.partner)
     for d in range(15):
-        landed(tb.at[d], rbs.at[d], at.partner)
         done = done + tb[d]
     quarter = jnp.zeros((16, 32), F32)
     for x in range(4):
@@ -570,11 +583,10 @@
             v((256, width), F32),
             v((2, 4, 16, 640), F32), v((4, 16, 640), F32), v((4, 16, 640), F32),
             v((3, 16, 640), F32), v((4, 24, 128), F32), v((15, 24, 128), F32),
-            dma((2, 16)), dma((2, 16)), dma((2, 6)), dma((2, 6)), dma((2, 6)), dma((2, 6)),
-            dma((2, 16)), dma((2, 16)), dma((2, 4)), dma((2, 4)),
-            dma((2, 6)), dma((2, 6)), dma((2, 6)), dma((2, 6)),
-            dma((2, 16)), dma((2, 16)), dma, dma, dma((3,)), dma((3,)),
-            dma((15,)), dma((15,)), dma((13,)),
+            dma((2,)), dma((2, 4)), dma((2,)), dma((2, 6)), dma((2,)), dma((2, 6)),
+            dma((2,)), dma((2, 4)), dma((2,)), dma((2, 4)),
+            dma((2,)), dma((2, 6)), dma((2,)), dma((2, 6)),
+            dma((2,)), dma((2,)), dma, dma, dma, dma, dma, dma, dma((13,)),
         ],
         compiler_params=pltpu.CompilerParams(
             collective_id=0, has_side_effects=True, vmem_limit_bytes=49 << 20

time: 101 us -> 99 us (0.980)
  Pallas kernels: 98.8 us -> 96.5 us
    pallas_call x1, Pallas kernels: 93.8 us -> 91.5 us  [layer(): pl.pallas_call(layer_kernel, out_shape=(v((256, width), BF), v((256, widt...]
where the time goes in v6:
time: 99 us; the launch traced here: 97.2 us
  Pallas kernels  96.5 us (97%)
    pallas_call x1, Pallas kernels, layer(): pl.pallas_call(layer_kernel, out_shape=(v((256, width), BF), v((256, widt...  91.5 us
    pallas_call x1, Pallas kernels, store(): pl.pallas_call(store_kernel, out_shape=tuple((jax.ShapeDtypeStruct(a.shap...  5.01 us

profile of v6, /device:TPU:0, one launch (start us, length us, event | category | flops | bytes accessed | tf_op | source)
XLA Modules:
  0.0 97.2 jit_solution(13548461538892419406)
XLA Ops:
  0.6 91.5 %shard_map.153 = (bf16[256,4096]{1,0:T(8,128)(2,1)S(1)}, bf16[256,4096]{1,0:T(8,128)(2,1)S(1)}, f32[192,4096]{1,0:T(8,128)S(1)}, f32[192,4096]{1,0:T(8,128)S(1)}...) custom-call(bf16[256,4096]{1,0:T(8,128)(2,1)} %tok_h.1, bf16[256,4096]{1,0:T(8,128)(2,1)} %cot_h.1, ...), custom_call_target="tpu_custom_call" | custom-call | tf_op jit(solution)/shard_map/pallas_call | solution.py:559
  92.2 5.0 %shard_map.154 = (bf16[256,4096]{1,0:T(8,128)(2,1)}, bf16[256,4096]{1,0:T(8,128)(2,1)}, f32[192,4096]{1,0:T(8,128)}, f32[192,4096]{1,0:T(8,128)}, f32[192,4096]{...) custom-call(bf16[256,4096]{1,0:T(8,128)(2,1)S(1)} %get-tuple-element.21.refs_0_, ...), custom_call_target="tpu_custom_call" | custom-call | tf_op jit(solution)/shard_map/pallas_call | solution.py:611

commit v7 on v6

--- a/solution.py
+++ b/solution.py
@@ -83,7 +83,7 @@
     ).wait_recv()
 
 
-HOPS = [(i, j) for i in range(4) for j in (0, 1, 3, 2)]
+HOPS = [(i, j) for i in range(4) for j in (0, 2, 1, 3)]
 NT = (((1,), (1,)), ((), ()))
 TN = (((0,), (0,)), ((), ()))
 
@@ -133,7 +133,6 @@
     at = Spot()
     plane = at.plane_peers()
     column = at.column_peers()
-    greet(plane + column)
     loads = [
         pltpu.make_async_copy(a, b, loc.at[k])
         for k, (a, b) in enumerate([(cot_h, cot), (wg_h, wg), (wu_h, wu), (wd_h, wd)])
@@ -143,6 +142,7 @@
         cols = slice(1024 * k, 1024 * k + 1024)
         pieces.append(pltpu.make_async_copy(tok_h.at[:, cols], tok.at[:, cols], loc.at[9 + k]))
         pieces[k].start()
+    greet(plane + column)
 
     row = lax.broadcasted_iota(jnp.int32, (64, 16), 0)
     lane = lax.broadcasted_iota(jnp.int32, (64, 16), 1)
@@ -379,7 +379,7 @@
             sums = combine(kind, 0, i, extra)
             for x in range(4):
                 om[kind, i * 4 + x] = sums[4 * x : 4 * x + 4, :]
-            for j in (1, 3, 2, 0):
+            for j in (2, 1, 3, 0):
                 e = at.in_plane(i, j)
                 src = om.at[kind, i * 4 + lax.rem(at.x + j, 4)]
                 if i or j:
@@ -537,7 +537,7 @@
     def grad_tile(j, cols):
         tgr[:, cols] = (base[:, cols] + dot(select_t, ret[1, :, cols])).astype(BF)
 
-    tiles(8, 512, grad_tile)
+    tiles(4, 1024, grad_tile)
     done = ext[at.y]
     landed(tb, rbs, at.partner)
     for d in range(15):

time: 99 us -> 99 us (level)
  no operation moved by 1% of the time
where the time goes in v7:
time: 99 us; the launch traced here: 97.2 us
  Pallas kernels  96.6 us (98%)
    pallas_call x1, Pallas kernels, layer(): pl.pallas_call(layer_kernel, out_shape=(v((256, width), BF), v((256, widt...  91.6 us
    pallas_call x1, Pallas kernels, store(): pl.pallas_call(store_kernel, out_shape=tuple((jax.ShapeDtypeStruct(a.shap...  5.01 us

profile of v7, /device:TPU:0, one launch (start us, length us, event | category | flops | bytes accessed | tf_op | source)
XLA Modules:
  0.0 97.2 jit_solution(4317045738095802491)
XLA Ops:
  0.6 91.6 %shard_map.153 = (bf16[256,4096]{1,0:T(8,128)(2,1)S(1)}, bf16[256,4096]{1,0:T(8,128)(2,1)S(1)}, f32[192,4096]{1,0:T(8,128)S(1)}, f32[192,4096]{1,0:T(8,128)S(1)}...) custom-call(bf16[256,4096]{1,0:T(8,128)(2,1)} %tok_h.1, bf16[256,4096]{1,0:T(8,128)(2,1)} %cot_h.1, ...), custom_call_target="tpu_custom_call" | custom-call | tf_op jit(solution)/shard_map/pallas_call | solution.py:559
  92.2 5.0 %shard_map.154 = (bf16[256,4096]{1,0:T(8,128)(2,1)}, bf16[256,4096]{1,0:T(8,128)(2,1)}, f32[192,4096]{1,0:T(8,128)}, f32[192,4096]{1,0:T(8,128)}, f32[192,4096]{...) custom-call(bf16[256,4096]{1,0:T(8,128)(2,1)S(1)} %get-tuple-element.21.refs_0_, ...), custom_call_target="tpu_custom_call" | custom-call | tf_op jit(solution)/shard_map/pallas_call | solution.py:611
